TPU v7x, 32 devices: a whole 2x2x4 slice. The times are simulated.
32 devices in a mesh: seq: 4 (over x, core), dp: 8 (over z, y).
Axes of the slice: x: 2, y: 2, z: 4, core: 2. Of those that a mesh axis runs over, the one named last changes fastest.
Arguments:
- tokens: bfloat16 [8, 1280, 960], P('dp', 'seq'), may hold values from -6 to 6
- seg_ids: int32 [8, 1280], P('dp', 'seq'), may hold values from 0 to 4, as said below
- positions: int32 [8, 1280], P('dp', 'seq'), may hold values from 0 to 1279, as said below
- attn_gain: float32 [960], replicated, may hold values from 0.25 to 1.75
- w_query: bfloat16 [960, 960], replicated, may hold values from -0.1875 to 0.1875
- w_key: bfloat16 [960, 320], replicated, may hold values from -0.1875 to 0.1875
- w_value: bfloat16 [960, 320], replicated, may hold values from -0.1875 to 0.1875
- w_out: bfloat16 [960, 960], replicated, may hold values from -0.5 to 0.5
- ffn_gain: float32 [960], replicated, may hold values from 0.25 to 1.75
- w_gate: bfloat16 [960, 2560], P(None, 'seq'), may hold values from -0.1875 to 0.1875
- w_up: bfloat16 [960, 2560], P(None, 'seq'), may hold values from -0.1875 to 0.1875
- w_down: bfloat16 [2560, 960], P('seq'), may hold values from -0.125 to 0.125
- cotangent: bfloat16 [8, 1280, 960], P('dp', 'seq'), may hold values from -6 to 6
Outputs:
- output: bfloat16 [8, 1280, 960], P('dp', 'seq')
- input_grad: float32 [8, 1280, 960], P('dp', 'seq')
- attn_gain_grad: float32 [960], P('dp')
- w_query_grad: float32 [960, 960], P('dp')
- w_key_grad: float32 [960, 320], P('dp')
- w_value_grad: float32 [960, 320], P('dp')
- w_out_grad: float32 [960, 960], P('dp')
- ffn_gain_grad: float32 [960], P('dp')
- w_gate_grad: float32 [960, 2560], P('dp', 'seq')
- w_up_grad: float32 [960, 2560], P('dp', 'seq')
- w_down_grad: float32 [2560, 960], P('seq', 'dp')
Inputs may be any that keep to these rules, and one draw needn't show every extreme that they name: `seg_ids`: within a row the ids start at 0 and never fall. `positions`: A token's position counts the tokens before it in its document (0 at a document's first token).
All inputs are finite; a program needn't handle non-finite values.
Results may differ from a plain program's by a relative error of at most 0.025.
Values may be sent and summed in bfloat16 or wider, within the bound.
A program may use at most 256 MiB of HBM per device.

v0:
```python
import functools

import jax
import jax.numpy as jnp
from jax import lax
from jax.experimental import pallas as pl
from jax.experimental.pallas import tpu as pltpu
from jax.sharding import PartitionSpec as P

MESH_ID = pl.DeviceIdType.MESH
HEADS = 15
KV_HEADS = 5
GROUP = 3
HEAD_DIM = 64
EPSILON = 1e-05
THETA = 10000.0
CHUNKS = 2
SHARES = 8
ROWS_PAD = 32
PIECE = 128
MASKED = -1e30
LOW = jnp.bfloat16
FULL = jnp.float32
SCALE = HEAD_DIM ** (-0.5)
NT = (((1,), (1,)), ((), ()))
TN = (((0,), (0,)), ((), ()))


def device(seq_pos, dp_pos):
    return {"seq": seq_pos, "dp": dp_pos}


def send(src, dst, send_sem, recv_sem, target, start=True):
    copy = pltpu.make_async_remote_copy(
        src_ref=src,
        dst_ref=dst,
        send_sem=send_sem,
        recv_sem=recv_sem,
        device_id=target,
        device_id_type=MESH_ID,
    )
    if start:
        copy.start()
    return copy


class Hops:
    def __init__(self, send_sem, recv_sem):
        self.send_sem, self.recv_sem, self.used = send_sem, recv_sem, 0

    def __call__(self, src, dst, target, start=True):
        index, self.used = self.used, self.used + 1
        return send(src, dst, self.send_sem.at[index], self.recv_sem.at[index], target, start)


class Later:
    def __init__(self, src, dst, sem):
        self.copy, self.dst, self.waited = pltpu.make_async_copy(src, dst, sem), dst, False
        self.copy.start()

    def __call__(self):
        if not self.waited:
            self.copy.wait()
            self.waited = True
        return self.dst


class Early:
    def __init__(self, sem):
        self.sem, self.copies = sem, []

    def __call__(self, src, dst, start=True):
        self.copies.append(pltpu.make_async_copy(src, dst, self.sem.at[len(self.copies)]))
        if start:
            self.copies[-1].start()
        return self.copies[-1]

    def finish(self):
        for copy in self.copies:
            copy.wait()


class LaterPairs:
    def __init__(self, key_hbm, value_hbm, dst, sem):
        self.copies, self.dst = [], dst
        for h in range(2 * KV_HEADS):
            src = (key_hbm, value_hbm)[h % 2].at[pl.ds(h // 2 * HEAD_DIM, HEAD_DIM)]
            self.copies.append(pltpu.make_async_copy(src, dst.at[pl.ds(h * HEAD_DIM, HEAD_DIM)], sem.at[h]))
            self.copies[-1].start()

    def __call__(self):
        for copy in self.copies:
            copy.wait()
        self.copies = []
        return self.dst


def greet(targets):
    barrier = pltpu.get_barrier_semaphore()
    for target in targets:
        pl.semaphore_signal(barrier, inc=1, device_id=target, device_id_type=MESH_ID)
    pl.semaphore_wait(barrier, len(targets))


def dot(left, right, dims=None):
    if dims is None:
        return jnp.dot(left, right, preferred_element_type=FULL)
    return lax.dot_general(left, right, dims, preferred_element_type=FULL)


def cost(microseconds):
    return pl.CostEstimate(flops=int(microseconds * 1.15e9), bytes_accessed=1 << 20, transcendentals=0)


def inverse_rms(value):
    return lax.rsqrt(jnp.mean(value * value, axis=-1, keepdims=True) + EPSILON)


def swap_halves(value):
    lane = lax.broadcasted_iota(jnp.int32, value.shape, 1)
    first = (lane & (HEAD_DIM // 2)) == 0
    return jnp.where(first, pltpu.roll(value, 96, 1), pltpu.roll(value, 32, 1))


def attn_forward_kernel(
    extra, res_ref, gains_ref, w_key_hbm, w_value_hbm, w_query_hbm, w_out_hbm, trig_hbm, place_ref, *rest
):
    if extra:
        extra_ref, extra_out = rest[0], rest[8]
        rest = rest[1:8] + rest[9:]
    normed_hbm, q_hbm, kv_hbm, log_out, mixed_out, after_out, normed_two_out, *rest = rest
    w_kv_buf, w_query_buf, w_out_buf, trig_buf, normed_out, q_out, kv_out, pair_sem, late_sem, early_sem, *rest = rest
    peak, total, acc, send_sem, recv_sem, *rest = rest
    w_kv = LaterPairs(w_key_hbm, w_value_hbm, w_kv_buf, pair_sem)
    trig = Later(trig_hbm, trig_buf, late_sem.at[0])
    w_query = Later(w_query_hbm, w_query_buf, late_sem.at[1])
    w_out = Later(w_out_hbm, w_out_buf, late_sem.at[2])
    early = Early(early_sem)
    seq, dp = lax.axis_index("seq"), lax.axis_index("dp")
    core, chip_x = lax.rem(seq, 2), lax.div(seq, 2)
    mate_seq, far_seq = seq + 1 - 2 * core, lax.rem(seq + 2, 4)
    mate, x_mate = device(mate_seq, dp), device(far_seq, dp)
    length = res_ref.shape[0]
    stacked = GROUP * length
    residual = res_ref[...].astype(FULL)
    normed_out[...] = (residual * inverse_rms(residual) * gains_ref[0:1, :]).astype(LOW)
    early(normed_out, normed_hbm)
    kv_width = 2 * KV_HEADS * HEAD_DIM
    kv_pre = dot(normed_out[...], w_kv()[...], NT)
    trig_ref = trig()
    for g in range(KV_HEADS):
        part = kv_pre[:, g * 128 : (g + 1) * 128]
        turned = part * trig_ref[2] + swap_halves(part) * trig_ref[3]
        kv_out[seq, :, g * 128 : (g + 1) * 128] = turned.astype(LOW)
    greet([mate, x_mate])
    own_kv = kv_out.at[seq]
    to_mate = send(own_kv, own_kv, send_sem.at[0], recv_sem.at[0], mate)
    to_x = send(own_kv, own_kv, send_sem.at[1], recv_sem.at[1], x_mate)
    q_pre = dot(normed_out[...], w_query()[...])
    lane = lax.broadcasted_iota(jnp.int32, (length, 128), 1)
    for pair in range((HEADS + 1) // 2):
        width = min(128, HEADS * HEAD_DIM - pair * 128)
        part = q_pre[:, pair * 128 : pair * 128 + width]
        if width < 128:
            part = jnp.concatenate([part, part], axis=1)
        turned = (part * trig_ref[0] + swap_halves(part) * trig_ref[1]) * SCALE
        q_out[2 * pair] = jnp.where(lane < HEAD_DIM, turned, 0.0).astype(LOW)
        if width == 128:
            q_out[2 * pair + 1] = jnp.where(lane < HEAD_DIM, pltpu.roll(turned, 64, 1), 0.0).astype(LOW)

    early(q_out, q_hbm)
    start, place = place_ref[0:1, :], place_ref[1:2, :]

    def attend(block, g):
        kv_g = kv_out[block, :, pl.ds(pl.multiple_of(g * 128, 128), 128)]
        q_g = q_out[pl.ds(3 * g, 3)].reshape(stacked, 128)
        scores = dot(kv_g, q_g, NT)
        key = lax.broadcasted_iota(jnp.int32, (length, stacked), 0) + block * length
        scores = jnp.where((key >= start) & (key <= place), scores, MASKED)
        new_peak = jnp.maximum(peak[g], jnp.max(scores, axis=0, keepdims=True))
        weights = jnp.exp(scores - new_peak)
        fade = jnp.exp(peak[g] - new_peak)
        total[g] = jnp.sum(weights, axis=0, keepdims=True) + fade * total[g]
        acc[g] = dot(kv_g, weights.astype(LOW), TN)[HEAD_DIM:] + fade * acc[g]
        peak[g] = new_peak

    peak[...] = jnp.full_like(peak, MASKED)
    total[...] = jnp.zeros_like(total)
    acc[...] = jnp.zeros_like(acc)
    far_kv, far_mate = kv_out.at[far_seq], lax.rem(mate_seq + 2, 4)
    hops = functools.partial(send, start=False)
    kv_onward = hops(far_kv, far_kv, send_sem.at[2], recv_sem.at[2], mate)
    starts = [kv_onward]
    if extra:
        mine, theirs = extra_out.at[seq], extra_out.at[far_seq]
        extra_x = hops(extra_ref, mine, send_sem.at[3], recv_sem.at[3], x_mate)
        extra_mate = hops(extra_ref, mine, send_sem.at[4], recv_sem.at[4], mate)
        starts += [early(extra_ref, mine, start=False), extra_x, extra_mate]
    kv_keep = early(kv_out, kv_hbm, start=False)

    @pl.loop(0, 4)
    def _(step):
        @pl.when(step == 1)
        def _():
            to_mate.wait()

        @pl.when(step == 2)
        def _():
            to_x.wait()
            for copy in starts:
                copy.start()

        @pl.when(step == 3)
        def _():
            kv_onward.wait()
            kv_keep.start()

        block = jnp.where(
            step == 0, seq, jnp.where(step == 1, mate_seq, jnp.where(step == 2, far_seq, far_mate))
        )

        @pl.when(block <= seq)
        def _():
            @pl.loop(0, KV_HEADS)
            def _(g):
                attend(block, g)

    if extra:
        extra_x.wait()
        extra_onward = send(theirs, theirs, send_sem.at[5], recv_sem.at[5], mate)
    for g in range(KV_HEADS):
        heads = (acc[g] / total[g]).T.astype(LOW)
        log_out[g] = peak[g] + jnp.log(total[g])
        for i in range(GROUP):
            h = GROUP * g + i
            mixed_out[:, h * HEAD_DIM : (h + 1) * HEAD_DIM] = heads[i * length : (i + 1) * length]
    after = residual + dot(mixed_out[...], w_out()[...])
    after_out[...] = after
    normed_two_out[...] = (after * inverse_rms(after) * gains_ref[1:2, :]).astype(LOW)
    if extra:
        extra_mate.wait()
        extra_onward.wait()
    early.finish()


VMEM = pl.BlockSpec(memory_space=pltpu.VMEM)
ANYWHERE = pl.BlockSpec(memory_space=pl.ANY)


def attn_forward(residual, gains, attn_weights, trig, place, extra=None):
    length, width = residual.shape
    kv_width = 2 * KV_HEADS * HEAD_DIM
    shapes = (
        ((length, width), LOW),
        ((HEADS, length, 128), LOW),
        ((4, length, kv_width), LOW),
        ((KV_HEADS, 1, GROUP * length), FULL),
        ((length, HEADS * HEAD_DIM), LOW),
        ((length, width), FULL),
        ((length, width), LOW),
    )
    args = (residual, gains) + tuple(attn_weights) + (trig, place)
    in_specs, out_specs, hops = [VMEM] * 2 + [ANYWHERE] * 5 + [VMEM], (ANYWHERE,) * 3 + (VMEM,) * 4, 3
    if extra is not None:
        args, in_specs, out_specs = args + (extra,), in_specs + [ANYWHERE], out_specs + (ANYWHERE,)
        shapes = shapes + (((4,) + extra.shape, extra.dtype),)
        hops = 6
    return pl.pallas_call(
        functools.partial(attn_forward_kernel, extra is not None),
        out_shape=tuple(jax.ShapeDtypeStruct(*s) for s in shapes),
        in_specs=in_specs,
        out_specs=out_specs,
        scratch_shapes=[
            pltpu.VMEM((kv_width, width), LOW),
            pltpu.VMEM(attn_weights[2].shape, LOW),
            pltpu.VMEM(attn_weights[3].shape, LOW),
            pltpu.VMEM(trig.shape, FULL),
            pltpu.VMEM((length, width), LOW),
            pltpu.VMEM((HEADS, length, 128), LOW),
            pltpu.VMEM((4, length, kv_width), LOW),
            pltpu.SemaphoreType.DMA((2 * KV_HEADS,)),
            pltpu.SemaphoreType.DMA((3,)),
            pltpu.SemaphoreType.DMA((4,)),
            pltpu.VMEM((KV_HEADS, 1, GROUP * length), FULL),
            pltpu.VMEM((KV_HEADS, 1, GROUP * length), FULL),
            pltpu.VMEM((KV_HEADS, HEAD_DIM, GROUP * length), FULL),
            pltpu.SemaphoreType.DMA((hops,)),
            pltpu.SemaphoreType.DMA((hops,)),
        ],
        compiler_params=pltpu.CompilerParams(
            collective_id=1 if residual.dtype == FULL else 0, has_side_effects=True, vmem_limit_bytes=60 * 1024 * 1024
        ),
        cost_estimate=cost(25),
        name="attn_forward",
    )(*args)


def prepare(positions):
    length = positions.shape[0]
    frequency = THETA ** (-(jnp.arange(HEAD_DIM // 2, dtype=FULL) * 2.0 / HEAD_DIM))
    angles = positions.astype(FULL)[:, None] * frequency
    cos, sin = jnp.cos(angles), jnp.sin(angles)
    one, none = jnp.ones((length, HEAD_DIM), FULL), jnp.zeros((length, HEAD_DIM), FULL)
    trig = jnp.stack(
        [
            jnp.concatenate([cos, cos, cos, cos], 1),
            jnp.concatenate([-sin, sin, -sin, sin], 1),
            jnp.concatenate([cos, cos, one], 1),
            jnp.concatenate([-sin, sin, none], 1),
        ]
    )
    own = lax.axis_index("seq") * length + jnp.arange(length, dtype=jnp.int32)
    place = jnp.stack([jnp.tile(own - positions, GROUP), jnp.tile(own, GROUP)])
    place = jnp.pad(place, ((0, 6), (0, 0)))
    return trig, place


def ffn_forward_kernel(
    after_hbm, normed_ref, w_gate_hbm, w_up_hbm, w_down_hbm,
    res_out, rows_hbm, pre_hbm,
    after_buf, w_gate_buf, w_up_buf, w_down_buf, rows_out, pre_out, late_sem, early_sem,
    mate_send, mate_recv, x_send, x_recv, own_far,
    send_sem, recv_sem,
):
    weights = [
        Later(src, dst, late_sem.at[i])
        for i, (src, dst) in enumerate(
            ((w_gate_hbm, w_gate_buf), (w_up_hbm, w_up_buf), (w_down_hbm, w_down_buf), (after_hbm, after_buf))
        )
    ]
    early = Early(early_sem)
    seq, dp = lax.axis_index("seq"), lax.axis_index("dp")
    core = lax.rem(seq, 2)
    mate_seq, far_seq = seq + 1 - 2 * core, lax.rem(seq + 2, 4)
    far_mate = lax.rem(mate_seq + 2, 4)
    mate, x_mate = device(mate_seq, dp), device(far_seq, dp)
    length = after_hbm.shape[0]
    step = length // CHUNKS
    greet([mate, x_mate])
    part = lambda k: pl.ds(k * step, step)

    def hop(index, src, dst, target):
        return send(src, dst, send_sem.at[index], recv_sem.at[index], target)

    rows_out[seq] = normed_ref[...]
    own_rows = lambda k: rows_out.at[seq, part(k)]
    far_rows = lambda k: rows_out.at[far_seq, part(k)]
    to_x = [hop(k, own_rows(k), own_rows(k), x_mate) for k in range(CHUNKS)]
    to_mate = hop(CHUNKS, rows_out.at[seq], rows_out.at[seq], mate)
    base = CHUNKS + 1
    w_gate_ref, w_up_ref, w_down_ref, after_ref = (weight() for weight in weights)

    def ffn(quarter, rows):
        block = rows_out[quarter, rows]
        gate = dot(block, w_gate_ref[...])
        up = dot(block, w_up_ref[...])
        pre_out[quarter, rows, : gate.shape[1]] = gate.astype(LOW)
        pre_out[quarter, rows, gate.shape[1] :] = up.astype(LOW)
        hidden = (gate * jax.nn.sigmoid(gate) * up).astype(LOW)
        return dot(hidden, w_down_ref[...], NT)

    everything = pl.ds(0, length)
    res_out[...] = after_ref[...] + ffn(seq, everything)
    to_mate.wait()
    mate_send[0] = ffn(mate_seq, everything).astype(LOW)
    back = hop(base, mate_send.at[0], mate_recv.at[0], mate)
    onward = []
    for k in range(CHUNKS):
        to_x[k].wait()
        onward.append(hop(base + 1 + k, far_rows(k), far_rows(k), mate))
        own_far[part(k)] = ffn(far_seq, part(k))
        onward[k].wait()
        mate_send[1, part(k)] = ffn(far_mate, part(k)).astype(LOW)
        joint = hop(base + 1 + CHUNKS + k, mate_send.at[1, part(k)], mate_recv.at[1, part(k)], mate)
        joint.wait()
        x_send[part(k)] = (own_far[part(k)] + mate_recv[1, part(k)].astype(FULL)).astype(LOW)
        onward.append(
            hop(base + 1 + 2 * CHUNKS + k, x_send.at[part(k)], x_recv.at[part(k)], x_mate)
        )
        onward[k], onward[-1] = onward[-1], onward[k]
        onward.pop()
    early(rows_out, rows_hbm)
    early(pre_out, pre_hbm)
    back.wait()
    res_out[...] += mate_recv[0].astype(FULL)
    for k in range(CHUNKS):
        onward[k].wait()
        res_out[part(k)] += x_recv[part(k)].astype(FULL)
    early.finish()


def ffn_forward(after, normed_two, w_gate, w_up, w_down):
    length, width = after.shape
    shapes = (
        ((length, width), FULL),
        ((4, length, width), LOW),
        ((4, length, 2 * w_gate.shape[1]), LOW),
    )
    sems = 3 * CHUNKS + CHUNKS + 2
    return pl.pallas_call(
        ffn_forward_kernel,
        out_shape=tuple(jax.ShapeDtypeStruct(*s) for s in shapes),
        in_specs=[ANYWHERE, VMEM] + [ANYWHERE] * 3,
        out_specs=(VMEM, ANYWHERE, ANYWHERE),
        scratch_shapes=[
            pltpu.VMEM((length, width), FULL),
            pltpu.VMEM(w_gate.shape, LOW),
            pltpu.VMEM(w_up.shape, LOW),
            pltpu.VMEM(w_down.shape, LOW),
            pltpu.VMEM((4, length, width), LOW),
            pltpu.VMEM((4, length, 2 * w_gate.shape[1]), LOW),
            pltpu.SemaphoreType.DMA((4,)),
            pltpu.SemaphoreType.DMA((2,)),
            pltpu.VMEM((2, length, width), LOW),
            pltpu.VMEM((2, length, width), LOW),
            pltpu.VMEM((length, width), LOW),
            pltpu.VMEM((length, width), LOW),
            pltpu.VMEM((length, width), FULL),
            pltpu.SemaphoreType.DMA((sems,)),
            pltpu.SemaphoreType.DMA((sems,)),
        ],
        compiler_params=pltpu.CompilerParams(
            collective_id=2, has_side_effects=True, vmem_limit_bytes=60 * 1024 * 1024
        ),
        cost_estimate=cost(36),
        name="ffn_forward",
    )(after, normed_two, w_gate, w_up, w_down)


def norm_back(value, gain, grad):
    inverse = inverse_rms(value)
    weighted = grad * gain
    inner = jnp.mean(weighted * value, axis=-1, keepdims=True)
    back = inverse * weighted - value * (inverse * inverse * inverse) * inner
    return back, jnp.sum(grad * value * inverse, axis=0, keepdims=True)


def ffn_all_kernel(second, reduce, up_ref, own_ref, after_hbm, gains_ref, still_refs, gate_ref, upw_ref, down_ref, far_ref, *rest):
    y_part = prev_hbm = pre_hbm = None
    if second:
        result_out, rest = rest[0], rest[1:]
    else:
        prev_hbm, pre_hbm, *rest = rest
    grad_out, gain_out, weight_hbm, *rest = rest
    if reduce:
        y_part, *rest = rest
    (
        w_in, w_down, still_ref, moved, in_grad, in_temp, hidden, back, after_buf, prev_buf, pre_buf, weight_out,
        load_sem, late_sem, early_sem, send_sem, recv_sem,
    ) = rest
    early = Early(early_sem)
    after_ref = Later(after_hbm, after_buf, late_sem.at[0])
    prev_ref = None if second else Later(prev_hbm, prev_buf, late_sem.at[1])
    pre_ref = None if second else Later(pre_hbm, pre_buf, late_sem.at[2])
    hop = Hops(send_sem, recv_sem)
    seq, dp = lax.axis_index("seq"), lax.axis_index("dp")
    core = lax.rem(seq, 2)
    mate_seq, far_seq = seq + 1 - 2 * core, lax.rem(seq + 2, 4)
    far_mate = lax.rem(mate_seq + 2, 4)
    mate, x_mate = device(mate_seq, dp), device(far_seq, dp)
    length, width = up_ref.shape
    units = gate_ref.shape[1]
    whole = pl.ds(0, width)

    def slots(w, rows):
        return w_in.at[w, rows, :units], w_in.at[w, rows, units:], w_down.at[w, rows]

    loads = []

    def load(src, dst):
        loads.append(pltpu.make_async_copy(src, dst, load_sem.at[len(loads)]))
        loads[-1].start()

    for src, dst in zip((gate_ref, upw_ref, down_ref), slots(0, whole)):
        load(src, dst)
    moved[seq] = own_ref[...].astype(LOW)
    at = 0
    for ref in still_refs:
        load(ref, still_ref.at[:, pl.ds(at, ref.shape[1])])
        at += ref.shape[1]
    far_from = len(loads)
    for d in range(SHARES):
        at = min(d * PIECE, width - PIECE)
        rows = min(PIECE, width - PIECE - at) if d == SHARES - 2 else PIECE
        for i, dst in enumerate(slots(2, pl.ds(at, rows))):
            load(far_ref.at[d, pl.ds(i * PIECE, rows)], dst)
    y_mate = device(seq, dp + 1 - 2 * lax.rem(dp, 2))
    greet([mate, x_mate] + ([y_mate] if reduce else []))
    mine, theirs = moved.at[seq], moved.at[far_seq]
    to_x = hop(mine, mine, x_mate)
    to_mate = hop(mine, mine, mate)
    beside = [hop(src, dst, mate) for src, dst in zip((gate_ref, upw_ref, down_ref), slots(1, whole))]
    rows_ref, low_ref = (moved, still_ref) if second else (still_ref, moved)

    def halves(quarter, w, grads, known=False):
        both = pre_buf[quarter].astype(FULL) if known else dot(rows_ref[quarter], w_in[w])
        gate, up = both[:, :units], both[:, units:]
        bend = jax.nn.sigmoid(gate)
        silu = gate * bend
        hidden_grad = dot(low_ref[quarter], w_down[w])
        grads[:, :units] = (hidden_grad * up * bend * (1.0 + gate * (1.0 - bend))).astype(LOW)
        grads[:, units:] = (hidden_grad * silu).astype(LOW)
        return (silu * up).astype(LOW)

    def local(w):
        act = halves(seq, w, in_temp)
        back[...] += dot(in_temp[...], w_in[w], NT)
        if second:
            grad_out[...] += dot(act, w_down[w], NT)

    for copy in loads[:far_from]:
        copy.wait()
    if not second:
        pre_ref()
    hidden[seq] = halves(seq, 0, in_grad.at[seq], not second)
    if second:
        back[...] = dot(in_grad[seq], w_in[0], NT)
        grad_out[...] = after_ref()[...] + dot(hidden[seq], w_down[0], NT)
    for copy in loads[far_from:]:
        copy.wait()
    across = [hop(w_in.at[2], w_in.at[3], mate), hop(w_down.at[2], w_down.at[3], mate)]
    for copy in beside:
        copy.wait()

    if second:

        @pl.loop(1, 4)
        def _(w):
            @pl.when(w == 3)
            def _():
                for copy in across:
                    copy.wait()

            local(w)

    else:
        back[...] = jnp.zeros_like(back)
        local(1)

    to_mate.wait()
    to_x.wait()
    onward = hop(theirs, theirs, mate)

    @pl.loop(0, 3)
    def _(i):
        @pl.when(i == 2)
        def _():
            onward.wait()

        quarter = jnp.where(i == 0, mate_seq, jnp.where(i == 1, far_seq, far_mate))
        hidden[quarter] = halves(quarter, 0, in_grad.at[quarter], not second)

    flat = lambda ref: ref[...].reshape(4 * length, ref.shape[2])
    share = width // SHARES

    def finish(i, term):
        for j in range(SHARES):
            rows = term[j * share : (j + 1) * share]
            if prev_ref is not None:
                rows = rows + prev_ref()[i, j // 2, j % 2].astype(FULL)
            weight_out[i, j // 2, j % 2] = rows.astype(LOW)
        early(weight_out.at[i], weight_hbm.at[i])

    def half(columns):
        return in_grad[:, :, columns].reshape(4 * length, units)

    if second:
        both = dot(flat(rows_ref), flat(in_grad), TN)
        finish(0, both[:, :units])
        finish(1, both[:, units:])
    else:
        finish(0, dot(flat(rows_ref), half(slice(0, units)), TN))
        if reduce:
            first_y = hop(weight_out.at[0, :, 1 - lax.rem(dp, 2)], y_part, y_mate)
        finish(1, dot(flat(rows_ref), half(slice(units, 2 * units)), TN))
        back[...] += dot(in_grad[seq], w_in[0], NT)
        for copy in across:
            copy.wait()

        @pl.loop(2, 4)
        def _(w):
            local(w)

    finish(2, dot(flat(low_ref), flat(hidden), TN))
    if second:
        result_out[...] = grad_out[...].astype(LOW)
    sent_back, gain_term = norm_back(after_ref()[...], gains_ref[1:2, :], back[...])
    grad_out[...] = up_ref[...].astype(FULL) + sent_back
    gain_out[...] = jnp.broadcast_to(gain_term, gain_out.shape)
    if reduce:
        first_y.wait()
    early.finish()


def ffn_all_call(stills, second, reduce, *refs):
    refs = refs if second else refs[:1] + refs
    return ffn_all_kernel(second, reduce, *refs[:4], refs[4 : 4 + stills], *refs[4 + stills :])


def ffn_all(second, reduce, upstream, own, after, gains, stills, weights, far, prev=None, pre=None):
    length, width = after.shape
    units = weights[0].shape[1]
    share = width // SHARES
    grads = (3, SHARES // 2, 2, share, units)
    shapes = (
        ((length, width), FULL),
        ((8, width), FULL),
        (grads, LOW),
    )
    if second:
        shapes = (((length, width), LOW),) + shapes
    if reduce:
        shapes = shapes + (((SHARES // 2, share, units), LOW),)
    args = (after, gains) + tuple(stills) + tuple(weights) + (far,)
    specs = [ANYWHERE, VMEM] + [ANYWHERE] * (len(stills) + 4)
    if second:
        args, specs = (upstream, own) + args, [VMEM, VMEM] + specs
    else:
        args, specs = (upstream,) + args, [VMEM] + specs
        args, specs = args + (prev, pre), specs + [ANYWHERE] * 2
    return pl.pallas_call(
        functools.partial(ffn_all_call, len(stills), second, reduce),
        out_shape=tuple(jax.ShapeDtypeStruct(*s) for s in shapes),
        in_specs=specs,
        out_specs=tuple(ANYWHERE if s[0] == grads else VMEM for s in shapes),
        scratch_shapes=[
            pltpu.VMEM((4, width, 2 * units), LOW),
            pltpu.VMEM((4, width, units), LOW),
            pltpu.VMEM((4, length, width), LOW),
            pltpu.VMEM((4, length, width), LOW),
            pltpu.VMEM((4, length, 2 * units), LOW),
            pltpu.VMEM((length, 2 * units), LOW),
            pltpu.VMEM((4, length, units), LOW),
            pltpu.VMEM((length, width), FULL),
            pltpu.VMEM((length, width), FULL),
            pltpu.VMEM((1, 1, 2, 8, 128) if second else grads, LOW),
            pltpu.VMEM((1, 8, 128) if second else pre.shape, LOW),
            pltpu.VMEM(grads, LOW),
            pltpu.SemaphoreType.DMA((3 + len(stills) + 3 * SHARES,)),
            pltpu.SemaphoreType.DMA((3,)),
            pltpu.SemaphoreType.DMA((3,)),
            pltpu.SemaphoreType.DMA((9,)),
            pltpu.SemaphoreType.DMA((9,)),
        ],
        compiler_params=pltpu.CompilerParams(
            collective_id=3 if second else 4, has_side_effects=True, vmem_limit_bytes=60 * 1024 * 1024
        ),
        cost_estimate=cost(30),
        name="ffn_second" if second else "ffn_first_backward",
    )(*args)


def attn_backward_kernel(
    last, after_grad_ref, w_out_ref, mixed_ref, gains_ref, place_ref, log_ref, q_hbm, kv_hbm, trig_hbm,
    res_hbm, normed_hbm, w_key_hbm, w_value_hbm, w_query_hbm, *rest
):
    if last:
        prev, ffn_ref, first_hbm, gain_ref = rest[:3], rest[3], rest[4], rest[5]
        grad_out, gain_out, ffn_out, share_outs = rest[6], rest[7], rest[8], rest[9:12]
        rest = rest[12:]
    else:
        prev = (None, None, None)
        grad_out, gain_out = rest[:2]
        part_hbms = rest[2:5]
        rest = rest[5:]
    q_buf, kv_buf, trig_buf, res_buf, normed_buf, w_kv_buf, w_query_buf, pair_sem, late_sem, early_sem, *rest = rest
    late = iter(late_sem.at[i] for i in range(11))
    q_later, kv_later = Later(q_hbm, q_buf, next(late)), Later(kv_hbm, kv_buf, next(late))
    mixed_grad, delta, kv_grad, query_grad, back, grad_send, grad_recv, send_sem, recv_sem = rest[:9]
    hop = Hops(send_sem, recv_sem)
    seq, dp = lax.axis_index("seq"), lax.axis_index("dp")
    core, chip_x = lax.rem(seq, 2), lax.div(seq, 2)
    mate_seq, far_seq = seq + 1 - 2 * core, lax.rem(seq + 2, 4)
    far_mate = lax.rem(mate_seq + 2, 4)
    mate, x_mate = device(mate_seq, dp), device(far_seq, dp)
    length, width = res_hbm.shape
    stacked = GROUP * length
    kv_width = 2 * KV_HEADS * HEAD_DIM
    parts = rest[9:12]
    if last:
        f_own, f_y_recv, f_a_send, f_a_recv, f_b_send, f_b_recv, gain_recv = rest[12:19]
        prev_bufs = rest[19:22]
        buffers = [rest[22 + 10 * i : 32 + 10 * i] for i in range(3)]
        row_y, row_z = lax.rem(dp, 2), lax.div(dp, 2)
        low_z, high_z = lax.rem(row_z, 2), lax.div(row_z, 2)
        y_mate = device(seq, dp + 1 - 2 * row_y)
        near_z = device(seq, dp + 2 - 4 * low_z)
        far_z = device(seq, dp + 4 - 8 * high_z)
        greet([mate, x_mate, y_mate, near_z, far_z])
        f_y = [hop(ffn_ref.at[m, :, 1 - row_y], f_y_recv.at[m], y_mate) for m in (1, 2)]
        first_y = Later(first_hbm, f_y_recv.at[0], next(late))
        own_shares = Later(ffn_ref.at[:, :, row_y], f_own, next(late))
        prev = [Later(src, dst, next(late)) for src, dst in zip(prev, prev_bufs)]
    else:
        greet([mate, x_mate])
    early = Early(early_sem)
    trig = Later(trig_hbm, trig_buf, next(late))
    normed_ref = Later(normed_hbm, normed_buf, next(late))
    w_query = Later(w_query_hbm, w_query_buf, next(late))
    w_kv = LaterPairs(w_key_hbm, w_value_hbm, w_kv_buf, pair_sem)
    res_ref = Later(res_hbm, res_buf, next(late))

    def near_fill(load, a_send):
        for h in range(2):
            a_send[h] = load(2 * h + 1 - low_z).astype(LOW)

    def far_fill(load, a_recv, b_send):
        b_send[...] = (load(2 - 2 * high_z + low_z) + a_recv[1 - high_z].astype(FULL)).astype(LOW)

    def z_total(load, a_recv, b_recv):
        return load(row_z) + a_recv[high_z].astype(FULL) + b_recv[...].astype(FULL)

    def f_load(m):
        return lambda z: own_shares()[m, z].astype(FULL) + f_y_recv[m, z].astype(FULL)

    if last:
        f_nears = [hop(f_a_send.at[m], f_a_recv.at[m], near_z, start=False) for m in range(3)]
        f_fars = [hop(f_b_send.at[m], f_b_recv.at[m], far_z, start=False) for m in range(3)]

    def f_near(m):
        own_shares()
        if m == 0:
            first_y()
        else:
            f_y[m - 1].wait()
        near_fill(f_load(m), f_a_send.at[m])
        f_nears[m].start()

    def f_far(m):
        f_nears[m].wait()
        far_fill(f_load(m), f_a_recv.at[m], f_b_send.at[m])
        f_fars[m].start()

    def f_finish(m):
        f_fars[m].wait()
        ffn_out[m] = z_total(f_load(m), f_a_recv.at[m], f_b_recv.at[m])

    quarter = lambda x, c: pl.ds(pl.multiple_of(64 * x + ROWS_PAD * c, ROWS_PAD), ROWS_PAD)

    def core_start(i):
        core_recv = buffers[i][0]
        return [hop(parts[i].at[:, quarter(x, 1 - core)], core_recv.at[x], mate) for x in range(2)]

    def x_make(i):
        return hop(*buffers[i][1:3], x_mate, start=False)

    def x_start(i, copies, x_copy):
        core_recv, x_send, x_recv = buffers[i][:3]
        for copy in copies:
            copy.wait()
        joint = parts[i][:, quarter(1 - chip_x, core)].astype(FULL) + core_recv[1 - chip_x].astype(FULL)
        x_send[...] = joint.astype(LOW)
        x_copy.start()
        return x_copy

    def y_start(i, copy):
        core_recv, x_send, x_recv, own, y_recv = buffers[i][:5]
        joint = parts[i][:, quarter(chip_x, core)].astype(FULL) + core_recv[chip_x].astype(FULL)
        copy.wait()
        own[...] = (joint + x_recv[...].astype(FULL)).astype(LOW).reshape(own.shape)
        return hop(own.at[:, 1 - row_y], y_recv, y_mate)

    def part_load(i):
        own, y_recv = buffers[i][3:5]
        return lambda z: own[z, row_y].astype(FULL) + y_recv[z].astype(FULL)

    def z_start(i, copy):
        copy.wait()
        near_fill(part_load(i), buffers[i][5])
        return hop(*buffers[i][5:7], near_z)

    def z_next(i, copy):
        copy.wait()
        far_fill(part_load(i), *buffers[i][6:8])
        return hop(*buffers[i][7:9], far_z)

    def share_start(i, copy):
        gathered = buffers[i][9]
        copy.wait()
        gathered[seq] = z_total(part_load(i), buffers[i][6], buffers[i][8]).astype(LOW)
        mine = gathered.at[seq]
        return hop(mine, mine, x_mate), hop(mine, mine, mate)

    def share_pass(i, copies):
        gathered = buffers[i][9]
        copies[0].wait()
        theirs = gathered.at[far_seq]
        return hop(theirs, theirs, mate), copies[1]

    def share_finish(i, copies):
        gathered = buffers[i][9]
        for copy in copies:
            copy.wait()
        for s in range(4):
            share_outs[i][s * ROWS_PAD : (s + 1) * ROWS_PAD] = gathered[s].astype(FULL)

    def weight(i, left, right):
        term = dot(left, right, TN)
        share = width // SHARES
        for j in range(SHARES):
            rows = term[j * share : (j + 1) * share]
            if prev[i] is not None:
                rows = rows + prev[i]()[j, :share].astype(FULL)
            parts[i][j, :share] = rows.astype(LOW)
        if not last:
            early(parts[i], part_hbms[i])

    low_grad = after_grad_ref[...].astype(LOW)
    mixed_back = dot(low_grad, w_out_ref[...], NT)
    lane = lax.broadcasted_iota(jnp.int32, (length, 128), 1)
    for pair in range((HEADS + 1) // 2):
        span = min(128, HEADS * HEAD_DIM - pair * 128)
        part = mixed_back[:, pair * 128 : pair * 128 + span]
        if span < 128:
            part = jnp.concatenate([part, part], axis=1)
        else:
            mixed_grad[2 * pair + 1] = jnp.where(lane >= HEAD_DIM, part, 0.0).astype(LOW)
        mixed_grad[2 * pair] = jnp.where(lane >= HEAD_DIM, pltpu.roll(part, 64, 1), 0.0).astype(LOW)
    product = mixed_back.astype(LOW).astype(FULL) * mixed_ref[...].astype(FULL)
    high = product.astype(LOW)
    rest_low = (product - high.astype(FULL)).astype(LOW)
    head = lax.broadcasted_iota(jnp.int32, (16, HEADS * HEAD_DIM), 0)
    column = lax.broadcasted_iota(jnp.int32, (16, HEADS * HEAD_DIM), 1)
    pick = jnp.where(lax.div(column, HEAD_DIM) == head, 1.0, 0.0).astype(LOW)
    sums = dot(pick, high, NT) + dot(pick, rest_low, NT)
    for g in range(KV_HEADS):
        delta[g] = jnp.concatenate([sums[3 * g + i : 3 * g + i + 1] for i in range(GROUP)], axis=1)
    query_grad[...] = jnp.zeros_like(query_grad)
    weight(0, mixed_ref[...], low_grad)
    if last:
        o_core = core_start(0)
        f_near(0)
        o_x = x_make(0)

    start, place = place_ref[0:1, :], place_ref[1:2, :]
    q_ref, kv_ref = q_later(), kv_later()

    def attend(block, g):
        columns = pl.ds(pl.multiple_of(g * 128, 128), 128)
        kv_g = kv_ref[block, :, columns]
        q_g = q_ref[pl.ds(3 * g, 3)].reshape(stacked, 128)
        out_g = mixed_grad[pl.ds(3 * g, 3)].reshape(stacked, 128)
        scores = dot(kv_g, q_g, NT)
        key = lax.broadcasted_iota(jnp.int32, (length, stacked), 0) + block * length
        weights = jnp.where((key >= start) & (key <= place), jnp.exp(scores - log_ref[g]), 0.0)
        probs_grad = dot(kv_g, out_g, NT)
        score_grad = (weights * (probs_grad - delta[g])).astype(LOW)
        kv_grad[block, :, columns] = dot(weights.astype(LOW), out_g) + dot(score_grad, q_g)
        query_grad[g] += dot(kv_g, score_grad, TN)[:HEAD_DIM]

    joint = hop(grad_send.at[0], grad_recv.at[0], mate, start=False)
    across = hop(grad_send.at[1], grad_recv.at[1], x_mate, start=False)
    beside = hop(grad_send.at[2], grad_recv.at[2], mate, start=False)

    @pl.loop(0, 4)
    def _(step):
        block = jnp.where(
            step == 0, far_mate, jnp.where(step == 1, far_seq, jnp.where(step == 2, mate_seq, seq))
        )

        @pl.when(block <= seq)
        def _():
            @pl.loop(0, KV_HEADS)
            def _(g):
                attend(block, g)

        @pl.when(block > seq)
        def _():
            kv_grad[block] = jnp.zeros_like(kv_grad[block])

        @pl.when(step == 0)
        def _():
            grad_send[0] = kv_grad[far_mate].astype(LOW)
            joint.start()

        @pl.when(step == 1)
        def _():
            joint.wait()
            grad_send[1] = (kv_grad[far_seq] + grad_recv[0].astype(FULL)).astype(LOW)
            across.start()
            if last:
                x_start(0, o_core, o_x)

        @pl.when(step == 2)
        def _():
            grad_send[2] = kv_grad[mate_seq].astype(LOW)
            beside.start()
            if last:
                f_far(0)
                f_near(1)

    trig_ref = trig()
    heads = []
    for g in range(KV_HEADS):
        turned = query_grad[g].T * SCALE
        heads += [turned[i * length : (i + 1) * length] for i in range(GROUP)]
    for pair in range((HEADS + 1) // 2):
        part = jnp.concatenate([heads[2 * pair], heads[min(2 * pair + 1, HEADS - 1)]], axis=1)
        turned = (part * trig_ref[0] - swap_halves(part) * trig_ref[1]).astype(LOW)
        at = kv_width + pair * 128
        stop = min(at + 128, kv_width + width)
        back[:, at:stop] = turned[:, : stop - at]
    weight(1, normed_ref()[...], back[:, kv_width:])
    if last:
        q_core = core_start(1)
        o_y = y_start(0, o_x)
    normed_grad = dot(back[:, kv_width:], w_query()[...], NT)
    if last:
        q_x = x_start(1, q_core, x_make(1))

    across.wait()
    beside.wait()
    own = kv_grad[seq] + grad_recv[1].astype(FULL) + grad_recv[2].astype(FULL)
    for g in range(KV_HEADS):
        part = own[:, g * 128 : (g + 1) * 128]
        back[:, g * 128 : (g + 1) * 128] = (part * trig_ref[2] - swap_halves(part) * trig_ref[3]).astype(LOW)
    weight(2, normed_ref()[...], back[:, :kv_width])
    if last:
        kv_core = core_start(2)
        f_far(1)
        f_near(2)
        kv_x = x_start(2, kv_core, x_make(2))
    normed_grad = normed_grad + dot(back[:, :kv_width], w_kv()[...])
    sent_back, gain_term = norm_back(res_ref()[...].astype(FULL), gains_ref[0:1, :], normed_grad)
    grad_out[...] = after_grad_ref[...] + sent_back
    if not last:
        gain_out[...] = jnp.broadcast_to(gain_term, gain_out.shape)
        early.finish()
        return

    row = lax.broadcasted_iota(jnp.int32, gain_out.shape, 0)
    gain_out[...] = gain_ref[...] + jnp.where(row == 0, gain_term, 0.0)
    partners = [mate, x_mate, y_mate, near_z, far_z]
    gain_hop = lambda n: hop(gain_out, gain_recv.at[n], partners[n])

    def gain_add(n, copy):
        copy.wait()
        gain_out[...] += gain_recv[n]

    gain_copy = gain_hop(0)
    f_finish(0)
    o_z = z_start(0, o_y)
    gain_add(0, gain_copy)
    gain_copy = gain_hop(1)
    q_y = y_start(1, q_x)
    f_far(2)
    f_finish(1)
    o_z = z_next(0, o_z)
    gain_add(1, gain_copy)
    gain_copy = gain_hop(2)
    kv_y = y_start(2, kv_x)
    q_z = z_start(1, q_y)
    gain_add(2, gain_copy)
    gain_copy = gain_hop(3)
    o_s = share_start(0, o_z)
    kv_z = z_start(2, kv_y)
    q_z = z_next(1, q_z)
    gain_add(3, gain_copy)
    gain_copy = gain_hop(4)
    f_finish(2)
    o_s = share_pass(0, o_s)
    kv_z = z_next(2, kv_z)
    q_s = share_start(1, q_z)
    gain_add(4, gain_copy)
    kv_s = share_start(2, kv_z)
    q_s = share_pass(1, q_s)
    share_finish(0, o_s)
    kv_s = share_pass(2, kv_s)
    share_finish(1, q_s)
    share_finish(2, kv_s)


def attn_backward(after_grad, residual, normed, gains, q, kv, log_total, mixed, attn_weights, trig, place, final=None):
    length, width = residual.shape
    kv_width = 2 * KV_HEADS * HEAD_DIM
    last = final is not None
    key_t, value_t, w_query, w_out = attn_weights
    args = (after_grad, w_out, mixed, gains, place, log_total, q, kv, trig, residual, normed, key_t, value_t, w_query)
    specs = [VMEM] * 6 + [ANYWHERE] * 8
    out_specs = (VMEM, VMEM)
    shapes = (((length, width), FULL), ((8, width), FULL))
    sizes = (width, width, kv_width)
    part_shapes = [((SHARES, 4 * ROWS_PAD, c), LOW) for c in sizes]
    scratch = [
        pltpu.VMEM(q.shape, LOW),
        pltpu.VMEM(kv.shape, LOW),
        pltpu.VMEM(trig.shape, FULL),
        pltpu.VMEM((length, width), residual.dtype),
        pltpu.VMEM((length, width), LOW),
        pltpu.VMEM((kv_width, width), LOW),
        pltpu.VMEM(w_query.shape, LOW),
        pltpu.SemaphoreType.DMA((2 * KV_HEADS,)),
        pltpu.SemaphoreType.DMA((11,)),
        pltpu.SemaphoreType.DMA((3,)),
        pltpu.VMEM((HEADS, length, 128), LOW),
        pltpu.VMEM((KV_HEADS, 1, GROUP * length), FULL),
        pltpu.VMEM((4, length, kv_width), FULL),
        pltpu.VMEM((KV_HEADS, HEAD_DIM, GROUP * length), FULL),
        pltpu.VMEM((length, kv_width + width), LOW),
        pltpu.VMEM((3, length, kv_width), LOW),
        pltpu.VMEM((3, length, kv_width), LOW),
    ]
    hops = 3
    if last:
        share, hidden = final[3].shape[3:]
        args = args + tuple(final)
        specs = specs + [ANYWHERE] * 5 + [VMEM]
        shapes = shapes + (((3, share, hidden), FULL),) + tuple(((4 * ROWS_PAD, c), FULL) for c in sizes)
        hops = 3 + 2 + 6 + 5 + 3 * (2 + 1 + 1 + 2 + 3)
        scratch += [pltpu.SemaphoreType.DMA((hops,))] * 2
        out_specs = (VMEM,) * len(shapes)
        scratch += [pltpu.VMEM(*s) for s in part_shapes]
        scratch += [
            pltpu.VMEM((3, 4, share, hidden), LOW),
            pltpu.VMEM((3, 4, share, hidden), LOW),
            pltpu.VMEM((3, 2, share, hidden), LOW),
            pltpu.VMEM((3, 2, share, hidden), LOW),
            pltpu.VMEM((3, share, hidden), LOW),
            pltpu.VMEM((3, share, hidden), LOW),
            pltpu.VMEM((5, 8, width), FULL),
        ]
        scratch += [pltpu.VMEM(*s) for s in part_shapes]
        for c in sizes:
            scratch += [
                pltpu.VMEM((2, SHARES, ROWS_PAD, c), LOW),
                pltpu.VMEM((SHARES, ROWS_PAD, c), LOW),
                pltpu.VMEM((SHARES, ROWS_PAD, c), LOW),
                pltpu.VMEM((4, 2, ROWS_PAD, c), LOW),
                pltpu.VMEM((4, ROWS_PAD, c), LOW),
                pltpu.VMEM((2, ROWS_PAD, c), LOW),
                pltpu.VMEM((2, ROWS_PAD, c), LOW),
                pltpu.VMEM((ROWS_PAD, c), LOW),
                pltpu.VMEM((ROWS_PAD, c), LOW),
                pltpu.VMEM((4, ROWS_PAD, c), LOW),
            ]
    else:
        shapes, out_specs = shapes + tuple(part_shapes), out_specs + (ANYWHERE,) * 3
        scratch += [pltpu.SemaphoreType.DMA((hops,))] * 2
        scratch += [pltpu.VMEM(*s) for s in part_shapes]
    return pl.pallas_call(
        functools.partial(attn_backward_kernel, last),
        out_shape=tuple(jax.ShapeDtypeStruct(*s) for s in shapes),
        in_specs=specs,
        out_specs=out_specs,
        scratch_shapes=scratch,
        compiler_params=pltpu.CompilerParams(
            collective_id=6 if last else 5, has_side_effects=True, vmem_limit_bytes=60 * 1024 * 1024
        ),
        cost_estimate=cost(95 if last else 40),
        name="attn_backward_last" if last else "attn_backward",
    )(*args)


def split_pairs(grads):
    rows = grads.shape[0]
    pairs = grads.reshape(rows, KV_HEADS, 2, HEAD_DIM)
    return pairs[:, :, 0].reshape(rows, -1), pairs[:, :, 1].reshape(rows, -1)


def on_device(
    tokens,
    seg_ids,
    positions,
    attn_gain,
    w_query,
    w_key,
    w_value,
    w_out,
    ffn_gain,
    w_gate,
    w_up,
    w_down,
    cotangent,
):
    width = tokens.shape[2]
    trig, place = prepare(positions[0])
    attn_weights = (w_key.T, w_value.T, w_query, w_out)
    gains = jnp.pad(jnp.stack([attn_gain, ffn_gain]), ((0, 6), (0, 0)))
    whole = lax.axis_size("dp") != SHARES
    share = width // SHARES
    own_weights = (w_gate, w_up, w_down.T)

    def over_x(value):
        return lax.ppermute(value, "seq", [(s, (s + 2) % 4) for s in range(4)])

    def over_rows_piece(value, d):
        return lax.dynamic_slice_in_dim(value, jnp.minimum(d * PIECE, width - PIECE), PIECE, axis=0)

    if whole:
        theirs = [over_x(w) for w in own_weights]
        far = jnp.stack([jnp.concatenate([over_rows_piece(w, d) for w in theirs]) for d in range(SHARES)])
    else:
        piece = jnp.concatenate([over_rows_piece(w, lax.axis_index("dp")) for w in own_weights])
        far = lax.all_gather(over_x(piece), "dp", axis=0)

    half = cotangent.shape[1] // 2
    first = attn_forward(tokens[0], gains, attn_weights, trig, place, cotangent[0, :half])
    residual, rows_all, pre_all = ffn_forward(first[5], first[6], *own_weights)
    second = attn_forward(residual, gains, attn_weights, trig, place, cotangent[0, half:])
    output, after_grad, ffn_gain_term, ffn_grads = ffn_all(
        True, False, cotangent[0], second[6], second[5], gains, (first[7], second[7]), own_weights, far
    )

    def attn_args(after_grad, residual, kept):
        normed, q, kv, log_total, mixed = kept[:5]
        return (after_grad, residual, normed, gains, q, kv, log_total, mixed, attn_weights, trig, place)

    upstream, attn_gain_term, *parts = attn_backward(*attn_args(after_grad, residual, second))
    gain_grads = jnp.stack([attn_gain_term[0], ffn_gain_term[0]])
    after_grad, ffn_gain_term, ffn_grads, *first_y = ffn_all(
        False, not whole, upstream, None, first[5], gains, (rows_all,), own_weights, far, ffn_grads, pre_all
    )
    args = attn_args(after_grad, tokens[0], first)
    if whole:
        upstream, attn_gain_term, *terms = attn_backward(*args)
        gain_grads = gain_grads + jnp.stack([attn_gain_term[0], ffn_gain_term[0]])
        parts = [part.astype(FULL) + term.astype(FULL) for part, term in zip(parts, terms)]
    else:
        gain_grads = gain_grads + jnp.stack([jnp.zeros_like(attn_gain), ffn_gain_term[0]])
        final = (*parts, ffn_grads, *first_y, jnp.pad(gain_grads, ((0, 6), (0, 0))))
        upstream, gain_all, ffn_share, *shares = attn_backward(*args, final)
    if whole:

        def over_rows(grads, dim):
            grads = lax.psum_scatter(grads.astype(LOW), "dp", scatter_dimension=dim, tiled=True)
            return grads.astype(FULL)

        def over_all(grads, dim):
            return lax.psum(over_rows(grads, dim).astype(LOW), "seq").astype(FULL)

        shares = [over_all(part[:, :share].reshape(width, -1), 0) for part in parts]
        ffn_share = over_rows(ffn_grads.reshape(3, width, -1), 1)
        own_gains = over_all(gain_grads, 1)
    else:
        shares = [part[:share] for part in shares]
        own_gains = lax.dynamic_slice_in_dim(gain_all, lax.axis_index("dp") * share, share, axis=1)
    key_share, value_share = split_pairs(shares[2])
    return (
        output[None],
        upstream[None],
        own_gains[0],
        shares[1],
        key_share,
        value_share,
        shares[0],
        own_gains[1],
        ffn_share[0],
        ffn_share[1],
        ffn_share[2].T,
    )


def solution(mesh):
    in_specs = (
        P("dp", "seq", None),
        P("dp", "seq"),
        P("dp", "seq"),
        P(),
        P(),
        P(),
        P(),
        P(),
        P(),
        P(None, "seq"),
        P(None, "seq"),
        P("seq", None),
        P("dp", "seq", None),
    )
    out_specs = (
        P("dp", "seq", None),
        P("dp", "seq", None),
        P("dp"),
        P("dp", None),
        P("dp", None),
        P("dp", None),
        P("dp", None),
        P("dp"),
        P("dp", "seq"),
        P("dp", "seq"),
        P("seq", "dp"),
    )
    return jax.shard_map(
        on_device, mesh=mesh, in_specs=in_specs, out_specs=out_specs, check_vma=False
    )
```

profile of v0, /device:TPU:0, one launch (start us, length us, event | category | flops | bytes accessed | tf_op | source)
XLA Modules:
  0.0 328.3 jit_solution(1683949082550862248)
XLA Ops:
  7.2 1.0 dynamic-slice_bitcast_fusion
  8.2 1.1 constant_dynamic-slice_fusion.1
  9.4 3.0 collective-permute-start
  15.1 0.9 pad_maximum_fusion.trig_hbm
  16.0 0.9 slice_bitcast_fusion
  16.8 6.8 %collective-permute-done = bf16[384,640]{1,0:T(8,128)(2,1)S(1)} collective-permute-done((bf16[384,640]{1,0:T(8,128)(2,1)S(1)}, bf16[384,640]{1,0:T(8,128)(2,1)S(1)}, u32[]{:S(2)}, u32[]{:S(2)}) %collective-permute-start) | collective-permute-done | bytes 491552 | tf_op jit(solution)/shard_map/ppermute | solution.py:1084
  23.6 0.8 copy-done.4
  24.4 29.4 %attn_forward.2 = (bf16[320,960]{1,0:T(8,128)(2,1)}, bf16[15,320,128]{2,1,0:T(8,128)(2,1)}, bf16[4,320,640]{2,1,0:T(8,128)(2,1)}, f32[5,1,960]{2,1,0:T(1,128)}, ...) custom-call(bf16[320,960]{1,0:T(8,128)(2,1)} %bitcast.52, ...), custom_call_target="tpu_custom_call" | custom-call | flops 28750000128 | bytes 1048576 | tf_op jit(solution)/shard_map/attn_forward/pallas_call | solution.py:268
  53.9 33.3 %ffn_forward.1 = (f32[320,960]{1,0:T(8,128)}, bf16[4,320,960]{2,1,0:T(8,128)(2,1)}, bf16[4,320,1280]{2,1,0:T(8,128)(2,1)}) custom-call(f32[320,960]{1,0:T(8,128)} %get-tuple-element.49.after_hbm.refs_1_, bf16[320,960]{1,0:T(8,128)(2,1)} %get-tuple-element.50.normed_ref, bf16[960,640]{1,0:T(8,128)(2,1)} %refs_4_.1, bf16[960,640]{1,0:T(8,128)(2,1)} %refs_5_.1, ...), custom_call_target="tpu_custom_call" | custom-call | flops 41400000512 | bytes 1048576 | tf_op jit(solution)/shard_map/ffn_forward/pallas_call | solution.py:400
  87.1 29.8 %attn_forward.3 = (bf16[320,960]{1,0:T(8,128)(2,1)}, bf16[15,320,128]{2,1,0:T(8,128)(2,1)}, bf16[4,320,640]{2,1,0:T(8,128)(2,1)}, f32[5,1,960]{2,1,0:T(1,128)}, ...) custom-call(f32[320,960]{1,0:T(8,128)} %get-tuple-element.51.res_ref.res, ...), custom_call_target="tpu_custom_call" | custom-call | flops 28750000128 | bytes 1048576 | tf_op jit(solution)/shard_map/attn_forward/pallas_call | solution.py:268
  117.0 32.5 %ffn_second.1 = (bf16[320,960]{1,0:T(8,128)(2,1)}, f32[320,960]{1,0:T(8,128)}, f32[8,960]{1,0:T(8,128)}, bf16[3,4,2,120,640]{4,3,2,1,0:T(8,128)(2,1)}) custom-call(bf16[320,960]{1,0:T(8,128)(2,1)} %bitcast.41, bf16[320,960]{1,0:T(8,128)(2,1)} %get-tuple-element.52.refs_1_, f32[320,960]{1,0:T(8,128)} %get-tuple-element.53.refs_2_, ...), custom_call_target="tpu_custom_call" | custom-call | flops 34500001792 | bytes 1048576 | tf_op jit(solution)/shard_map/ffn_second/pallas_call | solution.py:621
  149.5 0.8 slice.48
  150.2 34.0 %attn_backward.1 = (f32[320,960]{1,0:T(8,128)}, f32[8,960]{1,0:T(8,128)}, bf16[8,128,960]{2,1,0:T(8,128)(2,1)}, bf16[8,128,960]{2,1,0:T(8,128)(2,1)}, bf16[8,128,640]{2,1,0:T(8,128)(2,1)}) custom-call(f32[320,960]{1,0:T(8,128)} %get-tuple-element.57.after_grad_ref, bf16[960,960]{1,0:T(8,128)(2,1)} %w_out_ref.3, ...), custom_call_target="tpu_custom_call" | custom-call | flops 46000001024 | bytes 1048576 | tf_op jit(solution)/shard_map/attn_backward/pallas_call | solution.py:1040
  184.3 46.7 %ffn_first_backward.1 = (f32[320,960]{1,0:T(8,128)}, f32[8,960]{1,0:T(8,128)}, bf16[3,4,2,120,640]{4,3,2,1,0:T(8,128)(2,1)}, bf16[4,120,640]{2,1,0:T(8,128)(2,1)}) custom-call(f32[320,960]{1,0:T(8,128)} %get-tuple-element.63.refs_0_, f32[320,960]{1,0:T(8,128)} %get-tuple-element.49.after_hbm.refs_1_, f32[8,960]{1,0:T(8,128)} %select_maximum_fusion.gains_ref.refs_3_.refs_2_, ...), custom_call_target="tpu_custom_call" | custom-call | flops 34500001792 | bytes 1048576 | tf_op jit(solution)/shard_map/ffn_first_backward/pallas_call | solution.py:621
  231.0 0.8 slice.49
  231.7 0.8 slice.47
  233.1 80.2 %attn_backward_last.1 = (f32[320,960]{1,0:T(8,128)}, f32[8,960]{1,0:T(8,128)}, f32[3,120,640]{2,1,0:T(8,128)}, f32[128,960]{1,0:T(8,128)}, f32[128,960]{1,0:T(8,128)}, /*index=5*/f32[128,640]{1,0:T(8,128)}) custom-call(f32[320,960]{1,0:T(8,128)} %get-tuple-element.67.after_grad_ref, bf16[960,960]{1,0:T(8,128)(2,1)} %w_out_ref.3, ...), custom_call_target="tpu_custom_call" | custom-call | flops 109250002944 | bytes 1048576 | tf_op jit(solution)/shard_map/attn_backward_last/pallas_call | solution.py:1040
  313.4 0.8 constant_dynamic-slice_fusion
  314.7 1.0 slice.52
  316.7 0.8 slice.51
  317.5 0.8 slice.55
  318.4 0.9 slice_bitcast_fusion.2
  319.3 0.8 copy.28
  320.1 1.1 copy.29
  (45 shorter events, 4.9 us)
Async XLA Ops:
  7.2 5.2 %copy-start.7 = (s32[1,320]{1,0:T(1,128)S(1)}, s32[1,320]{1,0:T(1,128)}, u32[]{:S(2)}) copy-start(s32[1,320]{1,0:T(1,128)} %param.14) | copy-start | bytes 3844
  7.2 109.8 %all-gather.3.cloned.1.call-start = ((), (), s32[]{:S(2)}) async-start(), calls=%async_computation | async-start | bytes 4423680 | tf_op jit(solution)/shard_map/all_gather | solution.py:1094
  9.3 5.1 %copy-start.8 = (f32[960]{0:T(1024)S(1)}, f32[960]{0:T(1024)}, u32[]{:S(2)}) copy-start(f32[960]{0:T(1024)} %param.20) | copy-start | bytes 11524
  9.3 5.1 %copy-start.9 = (f32[960]{0:T(1024)S(1)}, f32[960]{0:T(1024)}, u32[]{:S(2)}) copy-start(f32[960]{0:T(1024)} %param.15) | copy-start | bytes 11524
  9.4 14.2 %collective-permute-start = (bf16[384,640]{1,0:T(8,128)(2,1)S(1)}, bf16[384,640]{1,0:T(8,128)(2,1)S(1)}, u32[]{:S(2)}, u32[]{:S(2)}) collective-permute-start(bf16[384,640]{1,0:T(8,128)(2,1)S(1)} %pad_maximum_fusion.1), channel_id=1, source_target_pairs={{0,16},{8,24},{16,0},{24,8},{1,17},{9,25},{17,1},{25,9},{2,18},{10... | collective-permute-start | bytes 1474568 | tf_op jit(solution)/shard_map/ppermute | solution.py:1084
  13.5 2.5 copy-start.2
  23.6 0.8 copy-start.4
  313.4 3.3 %copy-start.6 = (f32[128,960]{1,0:T(8,128)S(1)}, f32[128,960]{1,0:T(8,128)}, u32[]{:S(2)}) copy-start(f32[128,960]{1,0:T(8,128)} %get-tuple-element.83) | copy-start | bytes 1474564
  314.7 2.8 copy-start.5
  315.9 2.4 copy-start.1
  317.5 1.8 copy-start.3
  318.4 1.8 copy-start
Sparse Core Ops, SparseCore 0:
  24.5 71.5 all-gather.2
where the time goes:
time: 332 us; the launch traced here: 328 us
  Pallas kernels  286 us (86%)
  local copies, waits for them, and re-layouts  15.4 us (5%)
  between operations  14.5 us (4%)
  waiting for transfers between devices  6.81 us (2%)
    pallas_call x2, Pallas kernels, attn_backward(): pl.pallas_call(functools.partial(attn_backward_kernel, last), out_shape=t...  114 us
    pallas_call x2, Pallas kernels, ffn_all(): pl.pallas_call(functools.partial(ffn_all_call, len(stills), second, reduc...  79.2 us
    pallas_call x2, Pallas kernels, attn_forward(): pl.pallas_call(functools.partial(attn_forward_kernel, extra is not None),...  59.2 us
    pallas_call x1, Pallas kernels, ffn_forward(): pl.pallas_call(ffn_forward_kernel, out_shape=tuple((jax.ShapeDtypeStruct(...  33.3 us
    ppermute x1, waiting for transfers between devices, over_x(): return lax.ppermute(value, 'seq', [(s, (s + 2) % 4) for s in range(4)])  6.78 us
  transfers between devices with their start and end apart: 2, of which 1 were waited for; matrix products, arithmetic and copies ran while one was open for 1% of the time, Pallas kernels for 28%

commit v1 on v0

--- a/solution.py
+++ b/solution.py
@@ -122,177 +122,8 @@
     return jnp.where(first, pltpu.roll(value, 96, 1), pltpu.roll(value, 32, 1))
 
 
-def attn_forward_kernel(
-    extra, res_ref, gains_ref, w_key_hbm, w_value_hbm, w_query_hbm, w_out_hbm, trig_hbm, place_ref, *rest
-):
-    if extra:
-        extra_ref, extra_out = rest[0], rest[8]
-        rest = rest[1:8] + rest[9:]
-    normed_hbm, q_hbm, kv_hbm, log_out, mixed_out, after_out, normed_two_out, *rest = rest
-    w_kv_buf, w_query_buf, w_out_buf, trig_buf, normed_out, q_out, kv_out, pair_sem, late_sem, early_sem, *rest = rest
-    peak, total, acc, send_sem, recv_sem, *rest = rest
-    w_kv = LaterPairs(w_key_hbm, w_value_hbm, w_kv_buf, pair_sem)
-    trig = Later(trig_hbm, trig_buf, late_sem.at[0])
-    w_query = Later(w_query_hbm, w_query_buf, late_sem.at[1])
-    w_out = Later(w_out_hbm, w_out_buf, late_sem.at[2])
-    early = Early(early_sem)
-    seq, dp = lax.axis_index("seq"), lax.axis_index("dp")
-    core, chip_x = lax.rem(seq, 2), lax.div(seq, 2)
-    mate_seq, far_seq = seq + 1 - 2 * core, lax.rem(seq + 2, 4)
-    mate, x_mate = device(mate_seq, dp), device(far_seq, dp)
-    length = res_ref.shape[0]
-    stacked = GROUP * length
-    residual = res_ref[...].astype(FULL)
-    normed_out[...] = (residual * inverse_rms(residual) * gains_ref[0:1, :]).astype(LOW)
-    early(normed_out, normed_hbm)
-    kv_width = 2 * KV_HEADS * HEAD_DIM
-    kv_pre = dot(normed_out[...], w_kv()[...], NT)
-    trig_ref = trig()
-    for g in range(KV_HEADS):
-        part = kv_pre[:, g * 128 : (g + 1) * 128]
-        turned = part * trig_ref[2] + swap_halves(part) * trig_ref[3]
-        kv_out[seq, :, g * 128 : (g + 1) * 128] = turned.astype(LOW)
-    greet([mate, x_mate])
-    own_kv = kv_out.at[seq]
-    to_mate = send(own_kv, own_kv, send_sem.at[0], recv_sem.at[0], mate)
-    to_x = send(own_kv, own_kv, send_sem.at[1], recv_sem.at[1], x_mate)
-    q_pre = dot(normed_out[...], w_query()[...])
-    lane = lax.broadcasted_iota(jnp.int32, (length, 128), 1)
-    for pair in range((HEADS + 1) // 2):
-        width = min(128, HEADS * HEAD_DIM - pair * 128)
-        part = q_pre[:, pair * 128 : pair * 128 + width]
-        if width < 128:
-            part = jnp.concatenate([part, part], axis=1)
-        turned = (part * trig_ref[0] + swap_halves(part) * trig_ref[1]) * SCALE
-        q_out[2 * pair] = jnp.where(lane < HEAD_DIM, turned, 0.0).astype(LOW)
-        if width == 128:
-            q_out[2 * pair + 1] = jnp.where(lane < HEAD_DIM, pltpu.roll(turned, 64, 1), 0.0).astype(LOW)
-
-    early(q_out, q_hbm)
-    start, place = place_ref[0:1, :], place_ref[1:2, :]
-
-    def attend(block, g):
-        kv_g = kv_out[block, :, pl.ds(pl.multiple_of(g * 128, 128), 128)]
-        q_g = q_out[pl.ds(3 * g, 3)].reshape(stacked, 128)
-        scores = dot(kv_g, q_g, NT)
-        key = lax.broadcasted_iota(jnp.int32, (length, stacked), 0) + block * length
-        scores = jnp.where((key >= start) & (key <= place), scores, MASKED)
-        new_peak = jnp.maximum(peak[g], jnp.max(scores, axis=0, keepdims=True))
-        weights = jnp.exp(scores - new_peak)
-        fade = jnp.exp(peak[g] - new_peak)
-        total[g] = jnp.sum(weights, axis=0, keepdims=True) + fade * total[g]
-        acc[g] = dot(kv_g, weights.astype(LOW), TN)[HEAD_DIM:] + fade * acc[g]
-        peak[g] = new_peak
-
-    peak[...] = jnp.full_like(peak, MASKED)
-    total[...] = jnp.zeros_like(total)
-    acc[...] = jnp.zeros_like(acc)
-    far_kv, far_mate = kv_out.at[far_seq], lax.rem(mate_seq + 2, 4)
-    hops = functools.partial(send, start=False)
-    kv_onward = hops(far_kv, far_kv, send_sem.at[2], recv_sem.at[2], mate)
-    starts = [kv_onward]
-    if extra:
-        mine, theirs = extra_out.at[seq], extra_out.at[far_seq]
-        extra_x = hops(extra_ref, mine, send_sem.at[3], recv_sem.at[3], x_mate)
-        extra_mate = hops(extra_ref, mine, send_sem.at[4], recv_sem.at[4], mate)
-        starts += [early(extra_ref, mine, start=False), extra_x, extra_mate]
-    kv_keep = early(kv_out, kv_hbm, start=False)
-
-    @pl.loop(0, 4)
-    def _(step):
-        @pl.when(step == 1)
-        def _():
-            to_mate.wait()
-
-        @pl.when(step == 2)
-        def _():
-            to_x.wait()
-            for copy in starts:
-                copy.start()
-
-        @pl.when(step == 3)
-        def _():
-            kv_onward.wait()
-            kv_keep.start()
-
-        block = jnp.where(
-            step == 0, seq, jnp.where(step == 1, mate_seq, jnp.where(step == 2, far_seq, far_mate))
-        )
-
-        @pl.when(block <= seq)
-        def _():
-            @pl.loop(0, KV_HEADS)
-            def _(g):
-                attend(block, g)
-
-    if extra:
-        extra_x.wait()
-        extra_onward = send(theirs, theirs, send_sem.at[5], recv_sem.at[5], mate)
-    for g in range(KV_HEADS):
-        heads = (acc[g] / total[g]).T.astype(LOW)
-        log_out[g] = peak[g] + jnp.log(total[g])
-        for i in range(GROUP):
-            h = GROUP * g + i
-            mixed_out[:, h * HEAD_DIM : (h + 1) * HEAD_DIM] = heads[i * length : (i + 1) * length]
-    after = residual + dot(mixed_out[...], w_out()[...])
-    after_out[...] = after
-    normed_two_out[...] = (after * inverse_rms(after) * gains_ref[1:2, :]).astype(LOW)
-    if extra:
-        extra_mate.wait()
-        extra_onward.wait()
-    early.finish()
-
-
 VMEM = pl.BlockSpec(memory_space=pltpu.VMEM)
 ANYWHERE = pl.BlockSpec(memory_space=pl.ANY)
-
-
-def attn_forward(residual, gains, attn_weights, trig, place, extra=None):
-    length, width = residual.shape
-    kv_width = 2 * KV_HEADS * HEAD_DIM
-    shapes = (
-        ((length, width), LOW),
-        ((HEADS, length, 128), LOW),
-        ((4, length, kv_width), LOW),
-        ((KV_HEADS, 1, GROUP * length), FULL),
-        ((length, HEADS * HEAD_DIM), LOW),
-        ((length, width), FULL),
-        ((length, width), LOW),
-    )
-    args = (residual, gains) + tuple(attn_weights) + (trig, place)
-    in_specs, out_specs, hops = [VMEM] * 2 + [ANYWHERE] * 5 + [VMEM], (ANYWHERE,) * 3 + (VMEM,) * 4, 3
-    if extra is not None:
-        args, in_specs, out_specs = args + (extra,), in_specs + [ANYWHERE], out_specs + (ANYWHERE,)
-        shapes = shapes + (((4,) + extra.shape, extra.dtype),)
-        hops = 6
-    return pl.pallas_call(
-        functools.partial(attn_forward_kernel, extra is not None),
-        out_shape=tuple(jax.ShapeDtypeStruct(*s) for s in shapes),
-        in_specs=in_specs,
-        out_specs=out_specs,
-        scratch_shapes=[
-            pltpu.VMEM((kv_width, width), LOW),
-            pltpu.VMEM(attn_weights[2].shape, LOW),
-            pltpu.VMEM(attn_weights[3].shape, LOW),
-            pltpu.VMEM(trig.shape, FULL),
-            pltpu.VMEM((length, width), LOW),
-            pltpu.VMEM((HEADS, length, 128), LOW),
-            pltpu.VMEM((4, length, kv_width), LOW),
-            pltpu.SemaphoreType.DMA((2 * KV_HEADS,)),
-            pltpu.SemaphoreType.DMA((3,)),
-            pltpu.SemaphoreType.DMA((4,)),
-            pltpu.VMEM((KV_HEADS, 1, GROUP * length), FULL),
-            pltpu.VMEM((KV_HEADS, 1, GROUP * length), FULL),
-            pltpu.VMEM((KV_HEADS, HEAD_DIM, GROUP * length), FULL),
-            pltpu.SemaphoreType.DMA((hops,)),
-            pltpu.SemaphoreType.DMA((hops,)),
-        ],
-        compiler_params=pltpu.CompilerParams(
-            collective_id=1 if residual.dtype == FULL else 0, has_side_effects=True, vmem_limit_bytes=60 * 1024 * 1024
-        ),
-        cost_estimate=cost(25),
-        name="attn_forward",
-    )(*args)
 
 
 def prepare(positions):
@@ -315,124 +146,268 @@
     return trig, place
 
 
-def ffn_forward_kernel(
-    after_hbm, normed_ref, w_gate_hbm, w_up_hbm, w_down_hbm,
-    res_out, rows_hbm, pre_hbm,
-    after_buf, w_gate_buf, w_up_buf, w_down_buf, rows_out, pre_out, late_sem, early_sem,
-    mate_send, mate_recv, x_send, x_recv, own_far,
-    send_sem, recv_sem,
-):
-    weights = [
-        Later(src, dst, late_sem.at[i])
-        for i, (src, dst) in enumerate(
-            ((w_gate_hbm, w_gate_buf), (w_up_hbm, w_up_buf), (w_down_hbm, w_down_buf), (after_hbm, after_buf))
-        )
-    ]
-    early = Early(early_sem)
-    seq, dp = lax.axis_index("seq"), lax.axis_index("dp")
-    core = lax.rem(seq, 2)
-    mate_seq, far_seq = seq + 1 - 2 * core, lax.rem(seq + 2, 4)
-    far_mate = lax.rem(mate_seq + 2, 4)
-    mate, x_mate = device(mate_seq, dp), device(far_seq, dp)
-    length = after_hbm.shape[0]
-    step = length // CHUNKS
-    greet([mate, x_mate])
-    part = lambda k: pl.ds(k * step, step)
-
-    def hop(index, src, dst, target):
-        return send(src, dst, send_sem.at[index], recv_sem.at[index], target)
-
-    rows_out[seq] = normed_ref[...]
-    own_rows = lambda k: rows_out.at[seq, part(k)]
-    far_rows = lambda k: rows_out.at[far_seq, part(k)]
-    to_x = [hop(k, own_rows(k), own_rows(k), x_mate) for k in range(CHUNKS)]
-    to_mate = hop(CHUNKS, rows_out.at[seq], rows_out.at[seq], mate)
-    base = CHUNKS + 1
-    w_gate_ref, w_up_ref, w_down_ref, after_ref = (weight() for weight in weights)
-
-    def ffn(quarter, rows):
-        block = rows_out[quarter, rows]
-        gate = dot(block, w_gate_ref[...])
-        up = dot(block, w_up_ref[...])
-        pre_out[quarter, rows, : gate.shape[1]] = gate.astype(LOW)
-        pre_out[quarter, rows, gate.shape[1] :] = up.astype(LOW)
-        hidden = (gate * jax.nn.sigmoid(gate) * up).astype(LOW)
-        return dot(hidden, w_down_ref[...], NT)
-
-    everything = pl.ds(0, length)
-    res_out[...] = after_ref[...] + ffn(seq, everything)
-    to_mate.wait()
-    mate_send[0] = ffn(mate_seq, everything).astype(LOW)
-    back = hop(base, mate_send.at[0], mate_recv.at[0], mate)
-    onward = []
-    for k in range(CHUNKS):
-        to_x[k].wait()
-        onward.append(hop(base + 1 + k, far_rows(k), far_rows(k), mate))
-        own_far[part(k)] = ffn(far_seq, part(k))
-        onward[k].wait()
-        mate_send[1, part(k)] = ffn(far_mate, part(k)).astype(LOW)
-        joint = hop(base + 1 + CHUNKS + k, mate_send.at[1, part(k)], mate_recv.at[1, part(k)], mate)
-        joint.wait()
-        x_send[part(k)] = (own_far[part(k)] + mate_recv[1, part(k)].astype(FULL)).astype(LOW)
-        onward.append(
-            hop(base + 1 + 2 * CHUNKS + k, x_send.at[part(k)], x_recv.at[part(k)], x_mate)
-        )
-        onward[k], onward[-1] = onward[-1], onward[k]
-        onward.pop()
-    early(rows_out, rows_hbm)
-    early(pre_out, pre_hbm)
-    back.wait()
-    res_out[...] += mate_recv[0].astype(FULL)
-    for k in range(CHUNKS):
-        onward[k].wait()
-        res_out[part(k)] += x_recv[part(k)].astype(FULL)
-    early.finish()
-
-
-def ffn_forward(after, normed_two, w_gate, w_up, w_down):
-    length, width = after.shape
-    shapes = (
-        ((length, width), FULL),
-        ((4, length, width), LOW),
-        ((4, length, 2 * w_gate.shape[1]), LOW),
-    )
-    sems = 3 * CHUNKS + CHUNKS + 2
-    return pl.pallas_call(
-        ffn_forward_kernel,
-        out_shape=tuple(jax.ShapeDtypeStruct(*s) for s in shapes),
-        in_specs=[ANYWHERE, VMEM] + [ANYWHERE] * 3,
-        out_specs=(VMEM, ANYWHERE, ANYWHERE),
-        scratch_shapes=[
-            pltpu.VMEM((length, width), FULL),
-            pltpu.VMEM(w_gate.shape, LOW),
-            pltpu.VMEM(w_up.shape, LOW),
-            pltpu.VMEM(w_down.shape, LOW),
-            pltpu.VMEM((4, length, width), LOW),
-            pltpu.VMEM((4, length, 2 * w_gate.shape[1]), LOW),
-            pltpu.SemaphoreType.DMA((4,)),
-            pltpu.SemaphoreType.DMA((2,)),
-            pltpu.VMEM((2, length, width), LOW),
-            pltpu.VMEM((2, length, width), LOW),
-            pltpu.VMEM((length, width), LOW),
-            pltpu.VMEM((length, width), LOW),
-            pltpu.VMEM((length, width), FULL),
-            pltpu.SemaphoreType.DMA((sems,)),
-            pltpu.SemaphoreType.DMA((sems,)),
-        ],
-        compiler_params=pltpu.CompilerParams(
-            collective_id=2, has_side_effects=True, vmem_limit_bytes=60 * 1024 * 1024
-        ),
-        cost_estimate=cost(36),
-        name="ffn_forward",
-    )(after, normed_two, w_gate, w_up, w_down)
-
-
 def norm_back(value, gain, grad):
     inverse = inverse_rms(value)
     weighted = grad * gain
     inner = jnp.mean(weighted * value, axis=-1, keepdims=True)
     back = inverse * weighted - value * (inverse * inverse * inverse) * inner
     return back, jnp.sum(grad * value * inverse, axis=0, keepdims=True)
+
+
+KEPT = 6
+CUT = 3
+
+
+def forward_kernel(
+    tokens_ref, gains_ref, place_ref, cotangent_hbm, w_key_hbm, w_value_hbm, w_query_hbm, w_out_hbm, trig_hbm,
+    w_gate_hbm, w_up_hbm, w_down_hbm, *rest
+):
+    first_hbm, (rows_hbm, pre_hbm, res_hbm), rest = rest[:KEPT], rest[KEPT : KEPT + 3], rest[KEPT + 3 :]
+    second_hbm, two_hbm, extra_outs, rest = rest[:KEPT], rest[KEPT], rest[KEPT + 1 : KEPT + 3], rest[KEPT + 3 :]
+    first, second, rest = rest[:KEPT], rest[KEPT : 2 * KEPT], rest[2 * KEPT :]
+    (
+        w_kv_buf, w_query_buf, w_out_buf, trig_buf, w_gate_buf, w_up_buf, w_down_buf,
+        two, rows, pre, res, peak, total, acc, mate_send, mate_recv, x_send, x_recv, own_far,
+        pair_sem, late_sem, early_sem, send_sem, recv_sem,
+    ) = rest
+    w_kv = LaterPairs(w_key_hbm, w_value_hbm, w_kv_buf, pair_sem)
+    trig, w_query, w_out, w_gate, w_up, w_down = [
+        Later(src, dst, late_sem.at[i])
+        for i, (src, dst) in enumerate(
+            (
+                (trig_hbm, trig_buf), (w_query_hbm, w_query_buf), (w_out_hbm, w_out_buf),
+                (w_gate_hbm, w_gate_buf), (w_up_hbm, w_up_buf), (w_down_hbm, w_down_buf),
+            )
+        )
+    ]
+    early, hop = Early(early_sem), Hops(send_sem, recv_sem)
+    seq, dp = lax.axis_index("seq"), lax.axis_index("dp")
+    core = lax.rem(seq, 2)
+    mate_seq, far_seq = seq + 1 - 2 * core, lax.rem(seq + 2, 4)
+    far_mate = lax.rem(mate_seq + 2, 4)
+    mate, x_mate = device(mate_seq, dp), device(far_seq, dp)
+    length = tokens_ref.shape[0]
+    stacked = GROUP * length
+    start, place = place_ref[0:1, :], place_ref[1:2, :]
+    step = length // CHUNKS
+    part = lambda k: pl.ds(k * step, step)
+
+    def attention(residual_ref, buffers, hbm, extra_ref, extra_out, meet):
+        normed, q, kv, log_total, mixed, after = buffers
+        residual = residual_ref[...].astype(FULL)
+        normed[...] = (residual * inverse_rms(residual) * gains_ref[0:1, :]).astype(LOW)
+        early(normed, hbm[0])
+        kv_pre = dot(normed[...], w_kv()[...], NT)
+        trig_ref = trig()
+        for g in range(KV_HEADS):
+            piece = kv_pre[:, g * 128 : (g + 1) * 128]
+            turned = piece * trig_ref[2] + swap_halves(piece) * trig_ref[3]
+            kv[seq, :, g * 128 : (g + 1) * 128] = turned.astype(LOW)
+        if meet:
+            greet([mate, x_mate])
+        spans = (pl.ds(0, CUT * 128), pl.ds(CUT * 128, (KV_HEADS - CUT) * 128))
+        to_x = [hop(kv.at[seq, :, s], kv.at[seq, :, s], x_mate) for s in spans]
+        to_mate = hop(kv.at[seq], kv.at[seq], mate)
+        onward = [hop(kv.at[far_seq, :, s], kv.at[far_seq, :, s], mate, start=False) for s in spans]
+        mine, theirs = extra_out.at[seq], extra_out.at[far_seq]
+        extra = [early(extra_ref, mine, start=False)]
+        extra += [hop(extra_ref, mine, target, start=False) for target in (x_mate, mate)]
+        kv_keep = early(kv, hbm[2], start=False)
+        q_pre = dot(normed[...], w_query()[...])
+        lane = lax.broadcasted_iota(jnp.int32, (length, 128), 1)
+        for pair in range((HEADS + 1) // 2):
+            width = min(128, HEADS * HEAD_DIM - pair * 128)
+            piece = q_pre[:, pair * 128 : pair * 128 + width]
+            if width < 128:
+                piece = jnp.concatenate([piece, piece], axis=1)
+            turned = (piece * trig_ref[0] + swap_halves(piece) * trig_ref[1]) * SCALE
+            q[2 * pair] = jnp.where(lane < HEAD_DIM, turned, 0.0).astype(LOW)
+            if width == 128:
+                q[2 * pair + 1] = jnp.where(lane < HEAD_DIM, pltpu.roll(turned, 64, 1), 0.0).astype(LOW)
+        early(q, hbm[1])
+
+        def attend(block, g):
+            kv_g = kv[block, :, pl.ds(pl.multiple_of(g * 128, 128), 128)]
+            q_g = q[pl.ds(3 * g, 3)].reshape(stacked, 128)
+            scores = dot(kv_g, q_g, NT)
+            key = lax.broadcasted_iota(jnp.int32, (length, stacked), 0) + block * length
+            scores = jnp.where((key >= start) & (key <= place), scores, MASKED)
+            new_peak = jnp.maximum(peak[g], jnp.max(scores, axis=0, keepdims=True))
+            weights = jnp.exp(scores - new_peak)
+            fade = jnp.exp(peak[g] - new_peak)
+            total[g] = jnp.sum(weights, axis=0, keepdims=True) + fade * total[g]
+            acc[g] = dot(kv_g, weights.astype(LOW), TN)[HEAD_DIM:] + fade * acc[g]
+            peak[g] = new_peak
+
+        peak[...] = jnp.full_like(peak, MASKED)
+        total[...] = jnp.zeros_like(total)
+        acc[...] = jnp.zeros_like(acc)
+
+        @pl.loop(0, 6)
+        def _(turn):
+            @pl.when(turn == 1)
+            def _():
+                to_mate.wait()
+
+            @pl.when(turn == 2)
+            def _():
+                to_x[0].wait()
+                onward[0].start()
+                for copy in extra:
+                    copy.start()
+
+            @pl.when(turn == 3)
+            def _():
+                onward[0].wait()
+
+            @pl.when(turn == 4)
+            def _():
+                to_x[1].wait()
+                onward[1].start()
+
+            @pl.when(turn == 5)
+            def _():
+                onward[1].wait()
+                kv_keep.start()
+
+            block = jnp.where(
+                turn == 0, seq, jnp.where(turn == 1, mate_seq, jnp.where(lax.rem(turn, 2) == 0, far_seq, far_mate))
+            )
+            low = jnp.where(turn < 4, 0, CUT)
+            high = jnp.where((turn == 2) | (turn == 3), CUT, KV_HEADS)
+
+            @pl.when(block <= seq)
+            def _():
+                @pl.loop(low, high)
+                def _(g):
+                    attend(block, g)
+
+        for g in range(KV_HEADS):
+            heads = (acc[g] / total[g]).T.astype(LOW)
+            log_total[g] = peak[g] + jnp.log(total[g])
+            for i in range(GROUP):
+                h = GROUP * g + i
+                mixed[:, h * HEAD_DIM : (h + 1) * HEAD_DIM] = heads[i * length : (i + 1) * length]
+        early(log_total, hbm[3])
+        early(mixed, hbm[4])
+        extra[1].wait()
+        return hop(theirs, theirs, mate), extra[2]
+
+    def project(residual_ref, buffers, rows_of, two_ref):
+        mixed, after = buffers[4:]
+        value = residual_ref[rows_of].astype(FULL) + dot(mixed[rows_of], w_out()[...])
+        after[rows_of] = value
+        two_ref[rows_of] = (value * inverse_rms(value) * gains_ref[1:2, :]).astype(LOW)
+
+    waits = attention(tokens_ref, first, first_hbm, cotangent_hbm.at[pl.ds(0, step)], extra_outs[0], True)
+
+    to_x = []
+    for k in range(CHUNKS):
+        project(tokens_ref, first, part(k), rows.at[seq])
+        to_x.append(hop(rows.at[seq, part(k)], rows.at[seq, part(k)], x_mate))
+    to_mate = hop(rows.at[seq], rows.at[seq], mate)
+    early(first[5], first_hbm[5])
+    for copy in waits:
+        copy.wait()
+    w_gate_ref, w_up_ref, w_down_ref = w_gate(), w_up(), w_down()
+    units = w_gate_ref.shape[1]
+
+    def ffn(quarter, rows_of):
+        block = rows[quarter, rows_of]
+        gate = dot(block, w_gate_ref[...])
+        up = dot(block, w_up_ref[...])
+        pre[quarter, rows_of, :units] = gate.astype(LOW)
+        pre[quarter, rows_of, units:] = up.astype(LOW)
+        hidden = (gate * jax.nn.sigmoid(gate) * up).astype(LOW)
+        return dot(hidden, w_down_ref[...], NT)
+
+    everything = pl.ds(0, length)
+    res[...] = first[5][...] + ffn(seq, everything)
+    to_mate.wait()
+    mate_send[0] = ffn(mate_seq, everything).astype(LOW)
+    back = hop(mate_send.at[0], mate_recv.at[0], mate)
+    last = []
+    for k in range(CHUNKS):
+        to_x[k].wait()
+        onward = hop(rows.at[far_seq, part(k)], rows.at[far_seq, part(k)], mate)
+        own_far[part(k)] = ffn(far_seq, part(k))
+        onward.wait()
+        mate_send[1, part(k)] = ffn(far_mate, part(k)).astype(LOW)
+        joint = hop(mate_send.at[1, part(k)], mate_recv.at[1, part(k)], mate)
+        joint.wait()
+        x_send[part(k)] = (own_far[part(k)] + mate_recv[1, part(k)].astype(FULL)).astype(LOW)
+        last.append(hop(x_send.at[part(k)], x_recv.at[part(k)], x_mate))
+    early(rows, rows_hbm)
+    early(pre, pre_hbm)
+    back.wait()
+    res[...] += mate_recv[0].astype(FULL)
+    for k in range(CHUNKS):
+        last[k].wait()
+        res[part(k)] += x_recv[part(k)].astype(FULL)
+    early(res, res_hbm)
+
+    waits = attention(res, second, second_hbm, cotangent_hbm.at[pl.ds(step, step)], extra_outs[1], False)
+    project(res, second, everything, two)
+    early(second[5], second_hbm[5])
+    early(two, two_hbm)
+    for copy in waits:
+        copy.wait()
+    early.finish()
+
+
+def forward(tokens, gains, place, cotangent, attn_weights, trig, ffn_weights):
+    length, width = tokens.shape
+    kv_width = 2 * KV_HEADS * HEAD_DIM
+    stats = (KV_HEADS, 1, GROUP * length)
+    units = ffn_weights[0].shape[1]
+    kept = (
+        ((length, width), LOW),
+        ((HEADS, length, 128), LOW),
+        ((4, length, kv_width), LOW),
+        (stats, FULL),
+        ((length, HEADS * HEAD_DIM), LOW),
+        ((length, width), FULL),
+    )
+    middle = (((4, length, width), LOW), ((4, length, 2 * units), LOW), ((length, width), FULL))
+    extra = ((4, length // 2, width), LOW)
+    shapes = kept + middle + kept + (((length, width), LOW), extra, extra)
+    key_t, value_t, w_query, w_out = attn_weights
+    return pl.pallas_call(
+        forward_kernel,
+        out_shape=tuple(jax.ShapeDtypeStruct(*s) for s in shapes),
+        in_specs=[VMEM] * 3 + [ANYWHERE] * 9,
+        out_specs=(ANYWHERE,) * len(shapes),
+        scratch_shapes=[pltpu.VMEM(*s) for s in kept + kept]
+        + [
+            pltpu.VMEM((kv_width, width), LOW),
+            pltpu.VMEM(w_query.shape, LOW),
+            pltpu.VMEM(w_out.shape, LOW),
+            pltpu.VMEM(trig.shape, FULL),
+        ]
+        + [pltpu.VMEM(w.shape, LOW) for w in ffn_weights]
+        + [pltpu.VMEM((length, width), LOW)]
+        + [pltpu.VMEM(*s) for s in middle]
+        + [
+            pltpu.VMEM(stats, FULL),
+            pltpu.VMEM(stats, FULL),
+            pltpu.VMEM((KV_HEADS, HEAD_DIM, GROUP * length), FULL),
+            pltpu.VMEM((2, length, width), LOW),
+            pltpu.VMEM((2, length, width), LOW),
+            pltpu.VMEM((length, width), LOW),
+            pltpu.VMEM((length, width), LOW),
+            pltpu.VMEM((length, width), FULL),
+            pltpu.SemaphoreType.DMA((2 * KV_HEADS,)),
+            pltpu.SemaphoreType.DMA((6,)),
+            pltpu.SemaphoreType.DMA((18,)),
+            pltpu.SemaphoreType.DMA((26,)),
+            pltpu.SemaphoreType.DMA((26,)),
+        ],
+        compiler_params=pltpu.CompilerParams(
+            collective_id=0, has_side_effects=True, vmem_limit_bytes=60 * 1024 * 1024
+        ),
+        cost_estimate=cost(85),
+        name="forward",
+    )(tokens, gains, place, cotangent, *attn_weights, trig, *ffn_weights)
 
 
 def ffn_all_kernel(second, reduce, up_ref, own_ref, after_hbm, gains_ref, still_refs, gate_ref, upw_ref, down_ref, far_ref, *rest):
@@ -656,14 +631,14 @@
 ):
     if last:
         prev, ffn_ref, first_hbm, gain_ref = rest[:3], rest[3], rest[4], rest[5]
-        grad_out, gain_out, ffn_out, share_outs = rest[6], rest[7], rest[8], rest[9:12]
+        grad_hbm, gain_out, ffn_hbm, share_hbms = rest[6], rest[7], rest[8], rest[9:12]
         rest = rest[12:]
     else:
         prev = (None, None, None)
-        grad_out, gain_out = rest[:2]
+        grad_hbm, gain_out = rest[:2]
         part_hbms = rest[2:5]
         rest = rest[5:]
-    q_buf, kv_buf, trig_buf, res_buf, normed_buf, w_kv_buf, w_query_buf, pair_sem, late_sem, early_sem, *rest = rest
+    q_buf, kv_buf, trig_buf, res_buf, normed_buf, w_kv_buf, w_query_buf, grad_out, pair_sem, late_sem, early_sem, *rest = rest
     late = iter(late_sem.at[i] for i in range(11))
     q_later, kv_later = Later(q_hbm, q_buf, next(late)), Later(kv_hbm, kv_buf, next(late))
     mixed_grad, delta, kv_grad, query_grad, back, grad_send, grad_recv, send_sem, recv_sem = rest[:9]
@@ -680,14 +655,17 @@
     if last:
         f_own, f_y_recv, f_a_send, f_a_recv, f_b_send, f_b_recv, gain_recv = rest[12:19]
         prev_bufs = rest[19:22]
-        buffers = [rest[22 + 10 * i : 32 + 10 * i] for i in range(3)]
+        ffn_out, share_outs = rest[22], rest[23:26]
+        buffers = [rest[26 + 10 * i : 36 + 10 * i] for i in range(3)]
         row_y, row_z = lax.rem(dp, 2), lax.div(dp, 2)
         low_z, high_z = lax.rem(row_z, 2), lax.div(row_z, 2)
         y_mate = device(seq, dp + 1 - 2 * row_y)
         near_z = device(seq, dp + 2 - 4 * low_z)
         far_z = device(seq, dp + 4 - 8 * high_z)
-        greet([mate, x_mate, y_mate, near_z, far_z])
-        f_y = [hop(ffn_ref.at[m, :, 1 - row_y], f_y_recv.at[m], y_mate) for m in (1, 2)]
+        cross = device(far_mate, dp)
+        greet([mate, x_mate, cross, y_mate, near_z, far_z])
+        f_y = [None]
+        f_y += [hop(ffn_ref.at[m, :, 1 - row_y], f_y_recv.at[m], y_mate) for m in (1, 2)]
         first_y = Later(first_hbm, f_y_recv.at[0], next(late))
         own_shares = Later(ffn_ref.at[:, :, row_y], f_own, next(late))
         prev = [Later(src, dst, next(late)) for src, dst in zip(prev, prev_bufs)]
@@ -722,7 +700,7 @@
         if m == 0:
             first_y()
         else:
-            f_y[m - 1].wait()
+            f_y[m].wait()
         near_fill(f_load(m), f_a_send.at[m])
         f_nears[m].start()
 
@@ -734,6 +712,7 @@
     def f_finish(m):
         f_fars[m].wait()
         ffn_out[m] = z_total(f_load(m), f_a_recv.at[m], f_b_recv.at[m])
+        early(ffn_out.at[m], ffn_hbm.at[m])
 
     quarter = lambda x, c: pl.ds(pl.multiple_of(64 * x + ROWS_PAD * c, ROWS_PAD), ROWS_PAD)
 
@@ -779,13 +758,7 @@
         copy.wait()
         gathered[seq] = z_total(part_load(i), buffers[i][6], buffers[i][8]).astype(LOW)
         mine = gathered.at[seq]
-        return hop(mine, mine, x_mate), hop(mine, mine, mate)
-
-    def share_pass(i, copies):
-        gathered = buffers[i][9]
-        copies[0].wait()
-        theirs = gathered.at[far_seq]
-        return hop(theirs, theirs, mate), copies[1]
+        return [hop(mine, mine, target) for target in (x_mate, cross, mate)]
 
     def share_finish(i, copies):
         gathered = buffers[i][9]
@@ -793,6 +766,7 @@
             copy.wait()
         for s in range(4):
             share_outs[i][s * ROWS_PAD : (s + 1) * ROWS_PAD] = gathered[s].astype(FULL)
+        early(share_outs[i], share_hbms[i])
 
     def weight(i, left, right):
         term = dot(left, right, TN)
@@ -872,14 +846,14 @@
         def _():
             grad_send[0] = kv_grad[far_mate].astype(LOW)
             joint.start()
+            if last:
+                x_start(0, o_core, o_x)
 
         @pl.when(step == 1)
         def _():
             joint.wait()
             grad_send[1] = (kv_grad[far_seq] + grad_recv[0].astype(FULL)).astype(LOW)
             across.start()
-            if last:
-                x_start(0, o_core, o_x)
 
         @pl.when(step == 2)
         def _():
@@ -923,6 +897,7 @@
     normed_grad = normed_grad + dot(back[:, :kv_width], w_kv()[...])
     sent_back, gain_term = norm_back(res_ref()[...].astype(FULL), gains_ref[0:1, :], normed_grad)
     grad_out[...] = after_grad_ref[...] + sent_back
+    early(grad_out, grad_hbm)
     if not last:
         gain_out[...] = jnp.broadcast_to(gain_term, gain_out.shape)
         early.finish()
@@ -958,16 +933,14 @@
     gain_add(3, gain_copy)
     gain_copy = gain_hop(4)
     f_finish(2)
-    o_s = share_pass(0, o_s)
     kv_z = z_next(2, kv_z)
     q_s = share_start(1, q_z)
     gain_add(4, gain_copy)
     kv_s = share_start(2, kv_z)
-    q_s = share_pass(1, q_s)
     share_finish(0, o_s)
-    kv_s = share_pass(2, kv_s)
     share_finish(1, q_s)
     share_finish(2, kv_s)
+    early.finish()
 
 
 def attn_backward(after_grad, residual, normed, gains, q, kv, log_total, mixed, attn_weights, trig, place, final=None):
@@ -977,7 +950,7 @@
     key_t, value_t, w_query, w_out = attn_weights
     args = (after_grad, w_out, mixed, gains, place, log_total, q, kv, trig, residual, normed, key_t, value_t, w_query)
     specs = [VMEM] * 6 + [ANYWHERE] * 8
-    out_specs = (VMEM, VMEM)
+    out_specs = (ANYWHERE, VMEM)
     shapes = (((length, width), FULL), ((8, width), FULL))
     sizes = (width, width, kv_width)
     part_shapes = [((SHARES, 4 * ROWS_PAD, c), LOW) for c in sizes]
@@ -989,9 +962,10 @@
         pltpu.VMEM((length, width), LOW),
         pltpu.VMEM((kv_width, width), LOW),
         pltpu.VMEM(w_query.shape, LOW),
+        pltpu.VMEM((length, width), FULL),
         pltpu.SemaphoreType.DMA((2 * KV_HEADS,)),
         pltpu.SemaphoreType.DMA((11,)),
-        pltpu.SemaphoreType.DMA((3,)),
+        pltpu.SemaphoreType.DMA((7,)),
         pltpu.VMEM((HEADS, length, 128), LOW),
         pltpu.VMEM((KV_HEADS, 1, GROUP * length), FULL),
         pltpu.VMEM((4, length, kv_width), FULL),
@@ -1008,7 +982,7 @@
         shapes = shapes + (((3, share, hidden), FULL),) + tuple(((4 * ROWS_PAD, c), FULL) for c in sizes)
         hops = 3 + 2 + 6 + 5 + 3 * (2 + 1 + 1 + 2 + 3)
         scratch += [pltpu.SemaphoreType.DMA((hops,))] * 2
-        out_specs = (VMEM,) * len(shapes)
+        out_specs = out_specs + (ANYWHERE,) * 4
         scratch += [pltpu.VMEM(*s) for s in part_shapes]
         scratch += [
             pltpu.VMEM((3, 4, share, hidden), LOW),
@@ -1020,6 +994,7 @@
             pltpu.VMEM((5, 8, width), FULL),
         ]
         scratch += [pltpu.VMEM(*s) for s in part_shapes]
+        scratch += [pltpu.VMEM(*s) for s in shapes[2:]]
         for c in sizes:
             scratch += [
                 pltpu.VMEM((2, SHARES, ROWS_PAD, c), LOW),
@@ -1093,12 +1068,11 @@
         piece = jnp.concatenate([over_rows_piece(w, lax.axis_index("dp")) for w in own_weights])
         far = lax.all_gather(over_x(piece), "dp", axis=0)
 
-    half = cotangent.shape[1] // 2
-    first = attn_forward(tokens[0], gains, attn_weights, trig, place, cotangent[0, :half])
-    residual, rows_all, pre_all = ffn_forward(first[5], first[6], *own_weights)
-    second = attn_forward(residual, gains, attn_weights, trig, place, cotangent[0, half:])
+    results = forward(tokens[0], gains, place, cotangent[0], attn_weights, trig, own_weights)
+    first, (rows_all, pre_all, residual), results = results[:KEPT], results[KEPT : KEPT + 3], results[KEPT + 3 :]
+    second, normed_two, low_halves = results[:KEPT], results[KEPT], results[KEPT + 1 :]
     output, after_grad, ffn_gain_term, ffn_grads = ffn_all(
-        True, False, cotangent[0], second[6], second[5], gains, (first[7], second[7]), own_weights, far
+        True, False, cotangent[0], normed_two, second[5], gains, low_halves, own_weights, far
     )
 
     def attn_args(after_grad, residual, kept):

time: 332 us -> 324 us (0.976)
  Pallas kernels: 286 us -> 278 us
    pallas_call x3 -> x1, Pallas kernels: 92.5 us -> 79.5 us  [forward(): pl.pallas_call(forward_kernel, out_shape=tuple((jax.ShapeDtypeStruct(*s)...]
    pallas_call x2, Pallas kernels: 79.2 us -> 84.3 us  [ffn_all(): pl.pallas_call(functools.partial(ffn_all_call, len(stills), second, reduc...]
  transfers between devices with their start and end apart: 2 -> 2, of which waited for: 1 -> 1; matrix products, arithmetic and copies ran while one was open for 1% -> 1% of each run, Pallas kernels for 28% -> 25%
where the time goes in v1:
time: 324 us; the launch traced here: 320 us
  Pallas kernels  278 us (86%)
  local copies, waits for them, and re-layouts  14.5 us (4%)
  between operations  14.5 us (4%)
  waiting for transfers between devices  7.69 us (2%)
    pallas_call x2, Pallas kernels, attn_backward(): pl.pallas_call(functools.partial(attn_backward_kernel, last), out_shape=t...  114 us
    pallas_call x2, Pallas kernels, ffn_all(): pl.pallas_call(functools.partial(ffn_all_call, len(stills), second, reduc...  84.3 us
    pallas_call x1, Pallas kernels, forward(): pl.pallas_call(forward_kernel, out_shape=tuple((jax.ShapeDtypeStruct(*s)...  79.5 us
    ppermute x1, waiting for transfers between devices, over_x(): return lax.ppermute(value, 'seq', [(s, (s + 2) % 4) for s in range(4)])  7.66 us
  transfers between devices with their start and end apart: 2, of which 1 were waited for; matrix products, arithmetic and copies ran while one was open for 1% of the time, Pallas kernels for 25%

profile of v1, /device:TPU:0, one launch (start us, length us, event | category | flops | bytes accessed | tf_op | source)
XLA Modules:
  0.0 320.0 jit_solution(10905375172348524994)
XLA Ops:
  7.3 1.0 dynamic-slice_bitcast_fusion
  8.2 1.1 constant_dynamic-slice_fusion.1
  9.4 3.0 collective-permute-start
  12.7 0.6 multiply_cosine_fusion
  14.1 0.6 select_maximum_fusion.gains_ref.refs_3_.refs_2_
  15.1 0.9 pad_maximum_fusion.trig_hbm
  16.0 7.7 %collective-permute-done = bf16[384,640]{1,0:T(8,128)(2,1)S(1)} collective-permute-done((bf16[384,640]{1,0:T(8,128)(2,1)S(1)}, bf16[384,640]{1,0:T(8,128)(2,1)S(1)}, u32[]{:S(2)}, u32[]{:S(2)}) %collective-permute-start) | collective-permute-done | bytes 491552 | tf_op jit(solution)/shard_map/ppermute | solution.py:1059
  23.6 0.8 copy-done.3
  24.4 79.5 %forward.1 = (bf16[320,960]{1,0:T(8,128)(2,1)}, bf16[15,320,128]{2,1,0:T(8,128)(2,1)}, bf16[4,320,640]{2,1,0:T(8,128)(2,1)}, f32[5,1,960]{2,1,0:T(1,128)}, bf16[...) custom-call(bf16[320,960]{1,0:T(8,128)(2,1)} %bitcast.49, ...), custom_call_target="tpu_custom_call" | custom-call | flops 97749999616 | bytes 1048576 | tf_op jit(solution)/shard_map/forward/pallas_call | solution.py:375
  103.9 37.9 %ffn_second.1 = (bf16[320,960]{1,0:T(8,128)(2,1)}, f32[320,960]{1,0:T(8,128)}, f32[8,960]{1,0:T(8,128)}, bf16[3,4,2,120,640]{4,3,2,1,0:T(8,128)(2,1)}) custom-call(bf16[320,960]{1,0:T(8,128)(2,1)} %bitcast.48, bf16[320,960]{1,0:T(8,128)(2,1)} %get-tuple-element.48.refs_1_, f32[320,960]{1,0:T(8,128)} %get-tuple-element.49.refs_2_, ...), custom_call_target="tpu_custom_call" | custom-call | flops 34500001792 | bytes 1048576 | tf_op jit(solution)/shard_map/ffn_second/pallas_call | solution.py:596
  141.8 0.8 slice.40
  142.6 34.4 %attn_backward.1 = (f32[320,960]{1,0:T(8,128)}, f32[8,960]{1,0:T(8,128)}, bf16[8,128,960]{2,1,0:T(8,128)(2,1)}, bf16[8,128,960]{2,1,0:T(8,128)(2,1)}, bf16[8,128,640]{2,1,0:T(8,128)(2,1)}) custom-call(f32[320,960]{1,0:T(8,128)} %get-tuple-element.53.after_grad_ref, bf16[960,960]{1,0:T(8,128)(2,1)} %w_out_ref.3, ...), custom_call_target="tpu_custom_call" | custom-call | flops 46000001024 | bytes 1048576 | tf_op jit(solution)/shard_map/attn_backward/pallas_call | solution.py:1015
  177.0 46.5 %ffn_first_backward.1 = (f32[320,960]{1,0:T(8,128)}, f32[8,960]{1,0:T(8,128)}, bf16[3,4,2,120,640]{4,3,2,1,0:T(8,128)(2,1)}, bf16[4,120,640]{2,1,0:T(8,128)(2,1)}) custom-call(f32[320,960]{1,0:T(8,128)} %get-tuple-element.60.refs_0_, f32[320,960]{1,0:T(8,128)} %get-tuple-element.61.refs_1_, f32[8,960]{1,0:T(8,128)} %select_maximum_fusion.gains_ref.refs_3_.refs_2_, ...), custom_call_target="tpu_custom_call" | custom-call | flops 34500001792 | bytes 1048576 | tf_op jit(solution)/shard_map/ffn_first_backward/pallas_call | solution.py:596
  223.5 0.8 slice.41
  224.3 0.8 slice.39
  225.7 79.3 %attn_backward_last.1 = (f32[320,960]{1,0:T(8,128)}, f32[8,960]{1,0:T(8,128)}, f32[3,120,640]{2,1,0:T(8,128)}, f32[128,960]{1,0:T(8,128)}, f32[128,960]{1,0:T(8,128)}, /*index=5*/f32[128,640]{1,0:T(8,128)}) custom-call(f32[320,960]{1,0:T(8,128)} %get-tuple-element.65.after_grad_ref, bf16[960,960]{1,0:T(8,128)(2,1)} %w_out_ref.3, ...), custom_call_target="tpu_custom_call" | custom-call | flops 109250002944 | bytes 1048576 | tf_op jit(solution)/shard_map/attn_backward_last/pallas_call | solution.py:1015
  305.0 0.8 constant_dynamic-slice_fusion
  306.4 1.0 slice.44
  307.6 0.7 fusion.5
  308.3 0.8 slice.43
  309.2 0.8 slice.47
  310.0 0.9 slice_bitcast_fusion
  310.9 0.8 copy.28
  311.8 1.1 copy.29
  (40 shorter events, 2.8 us)
Async XLA Ops:
  7.2 5.2 %copy-start.6 = (s32[1,320]{1,0:T(1,128)S(1)}, s32[1,320]{1,0:T(1,128)}, u32[]{:S(2)}) copy-start(s32[1,320]{1,0:T(1,128)} %param.14) | copy-start | bytes 3844
  7.2 6.9 %copy-start.7 = (f32[960]{0:T(1024)S(1)}, f32[960]{0:T(1024)}, u32[]{:S(2)}) copy-start(f32[960]{0:T(1024)} %param.20) | copy-start | bytes 11524
  7.2 6.9 %copy-start.8 = (f32[960]{0:T(1024)S(1)}, f32[960]{0:T(1024)}, u32[]{:S(2)}) copy-start(f32[960]{0:T(1024)} %param.15) | copy-start | bytes 11524
  7.2 96.7 %all-gather.3.cloned.1.call-start = ((), (), s32[]{:S(2)}) async-start(), calls=%async_computation | async-start | bytes 4423680 | tf_op jit(solution)/shard_map/all_gather | solution.py:1069
  9.4 14.2 %collective-permute-start = (bf16[384,640]{1,0:T(8,128)(2,1)S(1)}, bf16[384,640]{1,0:T(8,128)(2,1)S(1)}, u32[]{:S(2)}, u32[]{:S(2)}) collective-permute-start(bf16[384,640]{1,0:T(8,128)(2,1)S(1)} %pad_maximum_fusion.1), channel_id=1, source_target_pairs={{0,16},{8,24},{16,0},{24,8},{1,17},{9,25},{17,1},{25,9},{2,18},{10... | collective-permute-start | bytes 1474568 | tf_op jit(solution)/shard_map/ppermute | solution.py:1059
  23.6 0.8 copy-start.3
  305.0 3.3 %copy-start.5 = (f32[128,960]{1,0:T(8,128)S(1)}, f32[128,960]{1,0:T(8,128)}, u32[]{:S(2)}) copy-start(f32[128,960]{1,0:T(8,128)} %get-tuple-element.81) | copy-start | bytes 1474564
  306.4 2.8 copy-start.4
  307.6 2.4 copy-start.1
  309.2 1.8 copy-start.2
  310.0 1.8 copy-start
Sparse Core Ops, SparseCore 0:
  24.5 71.5 all-gather.2

commit v2 on v1

--- a/solution.py
+++ b/solution.py
@@ -415,7 +415,7 @@
     if second:
         result_out, rest = rest[0], rest[1:]
     else:
-        prev_hbm, pre_hbm, *rest = rest
+        prev_hbm, pre_hbm, gain_ref, *rest = rest
     grad_out, gain_out, weight_hbm, *rest = rest
     if reduce:
         y_part, *rest = rest
@@ -561,7 +561,9 @@
         result_out[...] = grad_out[...].astype(LOW)
     sent_back, gain_term = norm_back(after_ref()[...], gains_ref[1:2, :], back[...])
     grad_out[...] = up_ref[...].astype(FULL) + sent_back
-    gain_out[...] = jnp.broadcast_to(gain_term, gain_out.shape)
+    row = lax.broadcasted_iota(jnp.int32, gain_out.shape, 0)
+    gain_term = jnp.where(row == 1, gain_term, 0.0)
+    gain_out[...] = gain_term if second else gain_ref[...] + gain_term
     if reduce:
         first_y.wait()
     early.finish()
@@ -572,7 +574,7 @@
     return ffn_all_kernel(second, reduce, *refs[:4], refs[4 : 4 + stills], *refs[4 + stills :])
 
 
-def ffn_all(second, reduce, upstream, own, after, gains, stills, weights, far, prev=None, pre=None):
+def ffn_all(second, reduce, upstream, own, after, gains, stills, weights, far, prev=None, pre=None, gain_grads=None):
     length, width = after.shape
     units = weights[0].shape[1]
     share = width // SHARES
@@ -592,7 +594,7 @@
         args, specs = (upstream, own) + args, [VMEM, VMEM] + specs
     else:
         args, specs = (upstream,) + args, [VMEM] + specs
-        args, specs = args + (prev, pre), specs + [ANYWHERE] * 2
+        args, specs = args + (prev, pre, gain_grads), specs + [ANYWHERE] * 2 + [VMEM]
     return pl.pallas_call(
         functools.partial(ffn_all_call, len(stills), second, reduce),
         out_shape=tuple(jax.ShapeDtypeStruct(*s) for s in shapes),
@@ -626,20 +628,23 @@
 
 
 def attn_backward_kernel(
-    last, after_grad_ref, w_out_ref, mixed_ref, gains_ref, place_ref, log_ref, q_hbm, kv_hbm, trig_hbm,
+    last, gain_ref, gains_ref, place_ref, log_ref, after_grad_hbm, w_out_hbm, mixed_hbm, q_hbm, kv_hbm, trig_hbm,
     res_hbm, normed_hbm, w_key_hbm, w_value_hbm, w_query_hbm, *rest
 ):
     if last:
-        prev, ffn_ref, first_hbm, gain_ref = rest[:3], rest[3], rest[4], rest[5]
-        grad_hbm, gain_out, ffn_hbm, share_hbms = rest[6], rest[7], rest[8], rest[9:12]
-        rest = rest[12:]
+        prev, ffn_ref, first_hbm = rest[:3], rest[3], rest[4]
+        grad_hbm, gain_out, ffn_hbm, share_hbms = rest[5], rest[6], rest[7], rest[8:11]
+        rest = rest[11:]
     else:
         prev = (None, None, None)
         grad_hbm, gain_out = rest[:2]
         part_hbms = rest[2:5]
         rest = rest[5:]
-    q_buf, kv_buf, trig_buf, res_buf, normed_buf, w_kv_buf, w_query_buf, grad_out, pair_sem, late_sem, early_sem, *rest = rest
-    late = iter(late_sem.at[i] for i in range(11))
+    q_buf, kv_buf, trig_buf, res_buf, normed_buf, w_kv_buf, w_query_buf, grad_out, after_grad_buf, w_out_buf, mixed_buf, pair_sem, late_sem, early_sem, *rest = rest
+    late = iter(late_sem.at[i] for i in range(14))
+    after_grad_later = Later(after_grad_hbm, after_grad_buf, next(late))
+    w_out_later = Later(w_out_hbm, w_out_buf, next(late))
+    mixed_later = Later(mixed_hbm, mixed_buf, next(late))
     q_later, kv_later = Later(q_hbm, q_buf, next(late)), Later(kv_hbm, kv_buf, next(late))
     mixed_grad, delta, kv_grad, query_grad, back, grad_send, grad_recv, send_sem, recv_sem = rest[:9]
     hop = Hops(send_sem, recv_sem)
@@ -779,6 +784,7 @@
         if not last:
             early(parts[i], part_hbms[i])
 
+    after_grad_ref, w_out_ref = after_grad_later(), w_out_later()
     low_grad = after_grad_ref[...].astype(LOW)
     mixed_back = dot(low_grad, w_out_ref[...], NT)
     lane = lax.broadcasted_iota(jnp.int32, (length, 128), 1)
@@ -790,6 +796,7 @@
         else:
             mixed_grad[2 * pair + 1] = jnp.where(lane >= HEAD_DIM, part, 0.0).astype(LOW)
         mixed_grad[2 * pair] = jnp.where(lane >= HEAD_DIM, pltpu.roll(part, 64, 1), 0.0).astype(LOW)
+    mixed_ref = mixed_later()
     product = mixed_back.astype(LOW).astype(FULL) * mixed_ref[...].astype(FULL)
     high = product.astype(LOW)
     rest_low = (product - high.astype(FULL)).astype(LOW)
@@ -898,13 +905,12 @@
     sent_back, gain_term = norm_back(res_ref()[...].astype(FULL), gains_ref[0:1, :], normed_grad)
     grad_out[...] = after_grad_ref[...] + sent_back
     early(grad_out, grad_hbm)
+    row = lax.broadcasted_iota(jnp.int32, gain_out.shape, 0)
+    gain_out[...] = gain_ref[...] + jnp.where(row == 0, gain_term, 0.0)
     if not last:
-        gain_out[...] = jnp.broadcast_to(gain_term, gain_out.shape)
         early.finish()
         return
 
-    row = lax.broadcasted_iota(jnp.int32, gain_out.shape, 0)
-    gain_out[...] = gain_ref[...] + jnp.where(row == 0, gain_term, 0.0)
     partners = [mate, x_mate, y_mate, near_z, far_z]
     gain_hop = lambda n: hop(gain_out, gain_recv.at[n], partners[n])
 
@@ -943,13 +949,14 @@
     early.finish()
 
 
-def attn_backward(after_grad, residual, normed, gains, q, kv, log_total, mixed, attn_weights, trig, place, final=None):
+def attn_backward(after_grad, residual, normed, gains, q, kv, log_total, mixed, attn_weights, trig, place, gain_grads, final=None):
     length, width = residual.shape
     kv_width = 2 * KV_HEADS * HEAD_DIM
     last = final is not None
     key_t, value_t, w_query, w_out = attn_weights
-    args = (after_grad, w_out, mixed, gains, place, log_total, q, kv, trig, residual, normed, key_t, value_t, w_query)
-    specs = [VMEM] * 6 + [ANYWHERE] * 8
+    args = (gain_grads, gains, place, log_total, after_grad, w_out, mixed, q, kv, trig, residual, normed)
+    args = args + (key_t, value_t, w_query)
+    specs = [VMEM] * 4 + [ANYWHERE] * 11
     out_specs = (ANYWHERE, VMEM)
     shapes = (((length, width), FULL), ((8, width), FULL))
     sizes = (width, width, kv_width)
@@ -963,8 +970,11 @@
         pltpu.VMEM((kv_width, width), LOW),
         pltpu.VMEM(w_query.shape, LOW),
         pltpu.VMEM((length, width), FULL),
+        pltpu.VMEM((length, width), FULL),
+        pltpu.VMEM(w_out.shape, LOW),
+        pltpu.VMEM(mixed.shape, LOW),
         pltpu.SemaphoreType.DMA((2 * KV_HEADS,)),
-        pltpu.SemaphoreType.DMA((11,)),
+        pltpu.SemaphoreType.DMA((14,)),
         pltpu.SemaphoreType.DMA((7,)),
         pltpu.VMEM((HEADS, length, 128), LOW),
         pltpu.VMEM((KV_HEADS, 1, GROUP * length), FULL),
@@ -978,7 +988,7 @@
     if last:
         share, hidden = final[3].shape[3:]
         args = args + tuple(final)
-        specs = specs + [ANYWHERE] * 5 + [VMEM]
+        specs = specs + [ANYWHERE] * 5
         shapes = shapes + (((3, share, hidden), FULL),) + tuple(((4 * ROWS_PAD, c), FULL) for c in sizes)
         hops = 3 + 2 + 6 + 5 + 3 * (2 + 1 + 1 + 2 + 3)
         scratch += [pltpu.SemaphoreType.DMA((hops,))] * 2
@@ -1071,28 +1081,24 @@
     results = forward(tokens[0], gains, place, cotangent[0], attn_weights, trig, own_weights)
     first, (rows_all, pre_all, residual), results = results[:KEPT], results[KEPT : KEPT + 3], results[KEPT + 3 :]
     second, normed_two, low_halves = results[:KEPT], results[KEPT], results[KEPT + 1 :]
-    output, after_grad, ffn_gain_term, ffn_grads = ffn_all(
+    output, after_grad, gain_grads, ffn_grads = ffn_all(
         True, False, cotangent[0], normed_two, second[5], gains, low_halves, own_weights, far
     )
 
-    def attn_args(after_grad, residual, kept):
+    def attn_args(after_grad, residual, kept, gain_grads):
         normed, q, kv, log_total, mixed = kept[:5]
-        return (after_grad, residual, normed, gains, q, kv, log_total, mixed, attn_weights, trig, place)
-
-    upstream, attn_gain_term, *parts = attn_backward(*attn_args(after_grad, residual, second))
-    gain_grads = jnp.stack([attn_gain_term[0], ffn_gain_term[0]])
-    after_grad, ffn_gain_term, ffn_grads, *first_y = ffn_all(
-        False, not whole, upstream, None, first[5], gains, (rows_all,), own_weights, far, ffn_grads, pre_all
+        return (after_grad, residual, normed, gains, q, kv, log_total, mixed, attn_weights, trig, place, gain_grads)
+
+    upstream, gain_grads, *parts = attn_backward(*attn_args(after_grad, residual, second, gain_grads))
+    after_grad, gain_grads, ffn_grads, *first_y = ffn_all(
+        False, not whole, upstream, None, first[5], gains, (rows_all,), own_weights, far, ffn_grads, pre_all, gain_grads
     )
-    args = attn_args(after_grad, tokens[0], first)
+    args = attn_args(after_grad, tokens[0], first, gain_grads)
     if whole:
-        upstream, attn_gain_term, *terms = attn_backward(*args)
-        gain_grads = gain_grads + jnp.stack([attn_gain_term[0], ffn_gain_term[0]])
+        upstream, gain_grads, *terms = attn_backward(*args)
         parts = [part.astype(FULL) + term.astype(FULL) for part, term in zip(parts, terms)]
     else:
-        gain_grads = gain_grads + jnp.stack([jnp.zeros_like(attn_gain), ffn_gain_term[0]])
-        final = (*parts, ffn_grads, *first_y, jnp.pad(gain_grads, ((0, 6), (0, 0))))
-        upstream, gain_all, ffn_share, *shares = attn_backward(*args, final)
+        upstream, gain_all, ffn_share, *shares = attn_backward(*args, (*parts, ffn_grads, *first_y))
     if whole:
 
         def over_rows(grads, dim):
@@ -1104,7 +1110,7 @@
 
         shares = [over_all(part[:, :share].reshape(width, -1), 0) for part in parts]
         ffn_share = over_rows(ffn_grads.reshape(3, width, -1), 1)
-        own_gains = over_all(gain_grads, 1)
+        own_gains = over_all(gain_grads[:2], 1)
     else:
         shares = [part[:share] for part in shares]
         own_gains = lax.dynamic_slice_in_dim(gain_all, lax.axis_index("dp") * share, share, axis=1)

time: 324 us -> 319 us (0.985)
  no operation moved by 1% of the time
where the time goes in v2:
time: 319 us; the launch traced here: 315 us
  Pallas kernels  275 us (86%)
  between operations  14.5 us (5%)
  local copies, waits for them, and re-layouts  11.6 us (4%)
  waiting for transfers between devices  7.69 us (2%)
    pallas_call x2, Pallas kernels, attn_backward(): pl.pallas_call(functools.partial(attn_backward_kernel, last), out_shape=t...  112 us
    pallas_call x2, Pallas kernels, ffn_all(): pl.pallas_call(functools.partial(ffn_all_call, len(stills), second, reduc...  84.3 us
    pallas_call x1, Pallas kernels, forward(): pl.pallas_call(forward_kernel, out_shape=tuple((jax.ShapeDtypeStruct(*s)...  79.5 us
    ppermute x1, waiting for transfers between devices, over_x(): return lax.ppermute(value, 'seq', [(s, (s + 2) % 4) for s in range(4)])  7.66 us
  transfers between devices with their start and end apart: 2, of which 1 were waited for; matrix products, arithmetic and copies ran while one was open for 1% of the time, Pallas kernels for 25%

profile of v2, /device:TPU:0, one launch (start us, length us, event | category | flops | bytes accessed | tf_op | source)
XLA Modules:
  0.0 315.0 jit_solution(3488815782258758160)
XLA Ops:
  7.3 1.0 dynamic-slice_bitcast_fusion
  8.2 1.1 constant_dynamic-slice_fusion.1
  9.4 3.0 collective-permute-start
  12.7 0.6 multiply_cosine_fusion
  13.5 0.6 pad.9.place_ref
  14.1 0.6 select_maximum_fusion.gains_ref.refs_3_.refs_2_
  14.8 0.3 maximum_bitcast_fusion
  15.1 0.9 pad_maximum_fusion.trig_hbm
  16.0 7.7 %collective-permute-done = bf16[384,640]{1,0:T(8,128)(2,1)S(1)} collective-permute-done((bf16[384,640]{1,0:T(8,128)(2,1)S(1)}, bf16[384,640]{1,0:T(8,128)(2,1)S(1)}, u32[]{:S(2)}, u32[]{:S(2)}) %collective-permute-start) | collective-permute-done | bytes 491552 | tf_op jit(solution)/shard_map/ppermute | solution.py:1069
  23.6 0.8 copy-done.3
  24.4 79.5 %forward.1 = (bf16[320,960]{1,0:T(8,128)(2,1)}, bf16[15,320,128]{2,1,0:T(8,128)(2,1)}, bf16[4,320,640]{2,1,0:T(8,128)(2,1)}, f32[5,1,960]{2,1,0:T(1,128)}, bf16[...) custom-call(bf16[320,960]{1,0:T(8,128)(2,1)} %bitcast.49, ...), custom_call_target="tpu_custom_call" | custom-call | flops 97749999616 | bytes 1048576 | tf_op jit(solution)/shard_map/forward/pallas_call | solution.py:375
  103.9 37.9 %ffn_second.1 = (bf16[320,960]{1,0:T(8,128)(2,1)}, f32[320,960]{1,0:T(8,128)}, f32[8,960]{1,0:T(8,128)}, bf16[3,4,2,120,640]{4,3,2,1,0:T(8,128)(2,1)}) custom-call(bf16[320,960]{1,0:T(8,128)(2,1)} %bitcast.48, bf16[320,960]{1,0:T(8,128)(2,1)} %get-tuple-element.48.refs_1_, f32[320,960]{1,0:T(8,128)} %get-tuple-element.49.refs_2_, ...), custom_call_target="tpu_custom_call" | custom-call | flops 34500001792 | bytes 1048576 | tf_op jit(solution)/shard_map/ffn_second/pallas_call | solution.py:598
  141.8 33.4 %attn_backward.1 = (f32[320,960]{1,0:T(8,128)}, f32[8,960]{1,0:T(8,128)}, bf16[8,128,960]{2,1,0:T(8,128)(2,1)}, bf16[8,128,960]{2,1,0:T(8,128)(2,1)}, bf16[8,128,640]{2,1,0:T(8,128)(2,1)}) custom-call(f32[8,960]{1,0:T(8,128)} %get-tuple-element.53.gain_ref, f32[8,960]{1,0:T(8,128)} %select_maximum_fusion.gains_ref.refs_3_.refs_2_, s32[8,960]{1,0:T(8,128)} %pad.9.place_ref, ...), custom_call_target="tpu_custom_call" | custom-call | flops 46000001024 | bytes 1048576 | tf_op jit(solution)/shard_map/attn_backward/pallas_call | solution.py:1025
  175.2 46.4 %ffn_first_backward.1 = (f32[320,960]{1,0:T(8,128)}, f32[8,960]{1,0:T(8,128)}, bf16[3,4,2,120,640]{4,3,2,1,0:T(8,128)(2,1)}, bf16[4,120,640]{2,1,0:T(8,128)(2,1)}) custom-call(f32[320,960]{1,0:T(8,128)} %get-tuple-element.61.refs_0_, f32[320,960]{1,0:T(8,128)} %get-tuple-element.62.refs_1_, f32[8,960]{1,0:T(8,128)} %select_maximum_fusion.gains_ref.refs_3_.refs_2_, ...), custom_call_target="tpu_custom_call" | custom-call | flops 34500001792 | bytes 1048576 | tf_op jit(solution)/shard_map/ffn_first_backward/pallas_call | solution.py:598
  221.7 78.3 %attn_backward_last.1 = (f32[320,960]{1,0:T(8,128)}, f32[8,960]{1,0:T(8,128)}, f32[3,120,640]{2,1,0:T(8,128)}, f32[128,960]{1,0:T(8,128)}, f32[128,960]{1,0:T(8,128)}, /*index=5*/f32[128,640]{1,0:T(8,128)}) custom-call(f32[8,960]{1,0:T(8,128)} %get-tuple-element.67.gain_ref, f32[8,960]{1,0:T(8,128)} %select_maximum_fusion.gains_ref.refs_3_.refs_2_, ...), custom_call_target="tpu_custom_call" | custom-call | flops 109250002944 | bytes 1048576 | tf_op jit(solution)/shard_map/attn_backward_last/pallas_call | solution.py:1025
  300.0 0.8 constant_dynamic-slice_fusion
  300.8 0.5 slice_bitcast_fusion.3
  301.3 1.0 slice.32
  302.6 0.7 fusion.5
  303.3 0.8 slice.31
  304.1 0.8 slice.35
  305.0 0.9 slice_bitcast_fusion
  305.9 0.8 copy.28
  306.8 1.1 copy.29
  (35 shorter events, 0.7 us)
Async XLA Ops:
  7.2 5.2 %copy-start.6 = (s32[1,320]{1,0:T(1,128)S(1)}, s32[1,320]{1,0:T(1,128)}, u32[]{:S(2)}) copy-start(s32[1,320]{1,0:T(1,128)} %param.14) | copy-start | bytes 3844
  7.2 6.9 %copy-start.7 = (f32[960]{0:T(1024)S(1)}, f32[960]{0:T(1024)}, u32[]{:S(2)}) copy-start(f32[960]{0:T(1024)} %param.20) | copy-start | bytes 11524
  7.2 6.9 %copy-start.8 = (f32[960]{0:T(1024)S(1)}, f32[960]{0:T(1024)}, u32[]{:S(2)}) copy-start(f32[960]{0:T(1024)} %param.15) | copy-start | bytes 11524
  7.2 96.7 %all-gather.3.cloned.1.call-start = ((), (), s32[]{:S(2)}) async-start(), calls=%async_computation | async-start | bytes 4423680 | tf_op jit(solution)/shard_map/all_gather | solution.py:1079
  9.4 14.2 %collective-permute-start = (bf16[384,640]{1,0:T(8,128)(2,1)S(1)}, bf16[384,640]{1,0:T(8,128)(2,1)S(1)}, u32[]{:S(2)}, u32[]{:S(2)}) collective-permute-start(bf16[384,640]{1,0:T(8,128)(2,1)S(1)} %pad_maximum_fusion.1), channel_id=1, source_target_pairs={{0,16},{8,24},{16,0},{24,8},{1,17},{9,25},{17,1},{25,9},{2,18},{10... | collective-permute-start | bytes 1474568 | tf_op jit(solution)/shard_map/ppermute | solution.py:1069
  23.6 0.8 copy-start.3
  300.0 3.3 %copy-start.5 = (f32[128,960]{1,0:T(8,128)S(1)}, f32[128,960]{1,0:T(8,128)}, u32[]{:S(2)}) copy-start(f32[128,960]{1,0:T(8,128)} %get-tuple-element.81) | copy-start | bytes 1474564
  301.3 2.8 copy-start.4
  302.6 2.4 copy-start.1
  304.1 1.8 copy-start.2
  305.0 1.8 copy-start
Sparse Core Ops, SparseCore 0:
  24.5 71.5 all-gather.2

commit v3 on v2

--- a/solution.py
+++ b/solution.py
@@ -425,7 +425,6 @@
     ) = rest
     early = Early(early_sem)
     after_ref = Later(after_hbm, after_buf, late_sem.at[0])
-    prev_ref = None if second else Later(prev_hbm, prev_buf, late_sem.at[1])
     pre_ref = None if second else Later(pre_hbm, pre_buf, late_sem.at[2])
     hop = Hops(send_sem, recv_sem)
     seq, dp = lax.axis_index("seq"), lax.axis_index("dp")
@@ -485,46 +484,6 @@
 
     for copy in loads[:far_from]:
         copy.wait()
-    if not second:
-        pre_ref()
-    hidden[seq] = halves(seq, 0, in_grad.at[seq], not second)
-    if second:
-        back[...] = dot(in_grad[seq], w_in[0], NT)
-        grad_out[...] = after_ref()[...] + dot(hidden[seq], w_down[0], NT)
-    for copy in loads[far_from:]:
-        copy.wait()
-    across = [hop(w_in.at[2], w_in.at[3], mate), hop(w_down.at[2], w_down.at[3], mate)]
-    for copy in beside:
-        copy.wait()
-
-    if second:
-
-        @pl.loop(1, 4)
-        def _(w):
-            @pl.when(w == 3)
-            def _():
-                for copy in across:
-                    copy.wait()
-
-            local(w)
-
-    else:
-        back[...] = jnp.zeros_like(back)
-        local(1)
-
-    to_mate.wait()
-    to_x.wait()
-    onward = hop(theirs, theirs, mate)
-
-    @pl.loop(0, 3)
-    def _(i):
-        @pl.when(i == 2)
-        def _():
-            onward.wait()
-
-        quarter = jnp.where(i == 0, mate_seq, jnp.where(i == 1, far_seq, far_mate))
-        hidden[quarter] = halves(quarter, 0, in_grad.at[quarter], not second)
-
     flat = lambda ref: ref[...].reshape(4 * length, ref.shape[2])
     share = width // SHARES
 
@@ -536,27 +495,82 @@
             weight_out[i, j // 2, j % 2] = rows.astype(LOW)
         early(weight_out.at[i], weight_hbm.at[i])
 
-    def half(columns):
-        return in_grad[:, :, columns].reshape(4 * length, units)
-
     if second:
+        hidden[seq] = halves(seq, 0, in_grad.at[seq])
+        back[...] = dot(in_grad[seq], w_in[0], NT)
+        grad_out[...] = after_ref()[...] + dot(hidden[seq], w_down[0], NT)
+    else:
+        pre_ref()
+
+        @pl.loop(0, 4)
+        def _(quarter):
+            both = pre_buf[quarter].astype(FULL)
+            gate = both[:, :units]
+            hidden[quarter] = (gate * jax.nn.sigmoid(gate) * both[:, units:]).astype(LOW)
+
+        halves(seq, 0, in_grad.at[seq], True)
+        back[...] = dot(in_grad[seq], w_in[0], NT)
+    if not second:
+        for copy in beside:
+            copy.wait()
+        local(1)
+    for copy in loads[far_from:]:
+        copy.wait()
+    across = [hop(w_in.at[2], w_in.at[3], mate), hop(w_down.at[2], w_down.at[3], mate)]
+    prev_ref = None if second else Later(prev_hbm, prev_buf, late_sem.at[1])
+    if second:
+        for copy in beside:
+            copy.wait()
+
+        @pl.loop(1, 4)
+        def _(w):
+            @pl.when(w == 3)
+            def _():
+                for copy in across:
+                    copy.wait()
+
+            local(w)
+
+    else:
+        local(2)
+
+    to_mate.wait()
+    if not second:
+        halves(mate_seq, 0, in_grad.at[mate_seq], True)
+    to_x.wait()
+    onward = hop(theirs, theirs, mate)
+    if second:
+
+        @pl.loop(0, 3)
+        def _(i):
+            @pl.when(i == 2)
+            def _():
+                onward.wait()
+
+            quarter = jnp.where(i == 0, mate_seq, jnp.where(i == 1, far_seq, far_mate))
+            hidden[quarter] = halves(quarter, 0, in_grad.at[quarter])
+
         both = dot(flat(rows_ref), flat(in_grad), TN)
         finish(0, both[:, :units])
         finish(1, both[:, units:])
+        finish(2, dot(flat(low_ref), flat(hidden), TN))
     else:
-        finish(0, dot(flat(rows_ref), half(slice(0, units)), TN))
+        onward.wait()
+        finish(2, dot(flat(low_ref), flat(hidden), TN))
         if reduce:
-            first_y = hop(weight_out.at[0, :, 1 - lax.rem(dp, 2)], y_part, y_mate)
-        finish(1, dot(flat(rows_ref), half(slice(units, 2 * units)), TN))
-        back[...] += dot(in_grad[seq], w_in[0], NT)
+            first_y = hop(weight_out.at[2, :, 1 - lax.rem(dp, 2)], y_part, y_mate)
+
+        @pl.loop(0, 2)
+        def _(i):
+            quarter = jnp.where(i == 0, far_seq, far_mate)
+            halves(quarter, 0, in_grad.at[quarter], True)
+
+        both = dot(flat(rows_ref), flat(in_grad), TN)
+        finish(0, both[:, :units])
+        finish(1, both[:, units:])
         for copy in across:
             copy.wait()
-
-        @pl.loop(2, 4)
-        def _(w):
-            local(w)
-
-    finish(2, dot(flat(low_ref), flat(hidden), TN))
+        local(3)
     if second:
         result_out[...] = grad_out[...].astype(LOW)
     sent_back, gain_term = norm_back(after_ref()[...], gains_ref[1:2, :], back[...])
@@ -669,9 +683,8 @@
         far_z = device(seq, dp + 4 - 8 * high_z)
         cross = device(far_mate, dp)
         greet([mate, x_mate, cross, y_mate, near_z, far_z])
-        f_y = [None]
-        f_y += [hop(ffn_ref.at[m, :, 1 - row_y], f_y_recv.at[m], y_mate) for m in (1, 2)]
-        first_y = Later(first_hbm, f_y_recv.at[0], next(late))
+        f_y = [hop(ffn_ref.at[m, :, 1 - row_y], f_y_recv.at[m], y_mate) for m in (0, 1)]
+        first_y = Later(first_hbm, f_y_recv.at[2], next(late))
         own_shares = Later(ffn_ref.at[:, :, row_y], f_own, next(late))
         prev = [Later(src, dst, next(late)) for src, dst in zip(prev, prev_bufs)]
     else:
@@ -702,7 +715,7 @@
 
     def f_near(m):
         own_shares()
-        if m == 0:
+        if m == 2:
             first_y()
         else:
             f_y[m].wait()
@@ -810,7 +823,7 @@
     weight(0, mixed_ref[...], low_grad)
     if last:
         o_core = core_start(0)
-        f_near(0)
+        f_near(2)
         o_x = x_make(0)
 
     start, place = place_ref[0:1, :], place_ref[1:2, :]
@@ -867,8 +880,8 @@
             grad_send[2] = kv_grad[mate_seq].astype(LOW)
             beside.start()
             if last:
-                f_far(0)
-                f_near(1)
+                f_far(2)
+                f_near(0)
 
     trig_ref = trig()
     heads = []
@@ -898,8 +911,8 @@
     weight(2, normed_ref()[...], back[:, :kv_width])
     if last:
         kv_core = core_start(2)
-        f_far(1)
-        f_near(2)
+        f_far(0)
+        f_near(1)
         kv_x = x_start(2, kv_core, x_make(2))
     normed_grad = normed_grad + dot(back[:, :kv_width], w_kv()[...])
     sent_back, gain_term = norm_back(res_ref()[...].astype(FULL), gains_ref[0:1, :], normed_grad)
@@ -919,13 +932,13 @@
         gain_out[...] += gain_recv[n]
 
     gain_copy = gain_hop(0)
-    f_finish(0)
+    f_finish(2)
     o_z = z_start(0, o_y)
     gain_add(0, gain_copy)
     gain_copy = gain_hop(1)
     q_y = y_start(1, q_x)
-    f_far(2)
-    f_finish(1)
+    f_far(1)
+    f_finish(0)
     o_z = z_next(0, o_z)
     gain_add(1, gain_copy)
     gain_copy = gain_hop(2)
@@ -938,7 +951,7 @@
     q_z = z_next(1, q_z)
     gain_add(3, gain_copy)
     gain_copy = gain_hop(4)
-    f_finish(2)
+    f_finish(1)
     kv_z = z_next(2, kv_z)
     q_s = share_start(1, q_z)
     gain_add(4, gain_copy)

time: 319 us -> 318 us (level)
  no operation moved by 1% of the time
where the time goes in v3:
time: 318 us; the launch traced here: 314 us
  Pallas kernels  274 us (86%)
  between operations  14.7 us (5%)
  local copies, waits for them, and re-layouts  11.6 us (4%)
  waiting for transfers between devices  7.69 us (2%)
    pallas_call x2, Pallas kernels, attn_backward(): pl.pallas_call(functools.partial(attn_backward_kernel, last), out_shape=t...  111 us
    pallas_call x2, Pallas kernels, ffn_all(): pl.pallas_call(functools.partial(ffn_all_call, len(stills), second, reduc...  83.2 us
    pallas_call x1, Pallas kernels, forward(): pl.pallas_call(forward_kernel, out_shape=tuple((jax.ShapeDtypeStruct(*s)...  79.5 us
    ppermute x1, waiting for transfers between devices, over_x(): return lax.ppermute(value, 'seq', [(s, (s + 2) % 4) for s in range(4)])  7.66 us
  transfers between devices with their start and end apart: 2, of which 1 were waited for; matrix products, arithmetic and copies ran while one was open for 1% of the time, Pallas kernels for 25%

profile of v3, /device:TPU:0, one launch (start us, length us, event | category | flops | bytes accessed | tf_op | source)
XLA Modules:
  0.0 313.6 jit_solution(955445144611054380)
XLA Ops:
  7.3 1.0 dynamic-slice_bitcast_fusion
  8.2 1.1 constant_dynamic-slice_fusion.1
  9.4 3.0 collective-permute-start
  12.7 0.6 multiply_cosine_fusion
  13.5 0.6 pad.9.place_ref
  14.1 0.6 select_maximum_fusion.gains_ref.refs_3_.refs_2_
  14.8 0.3 maximum_bitcast_fusion
  15.1 0.9 pad_maximum_fusion.trig_hbm
  16.0 7.7 %collective-permute-done = bf16[384,640]{1,0:T(8,128)(2,1)S(1)} collective-permute-done((bf16[384,640]{1,0:T(8,128)(2,1)S(1)}, bf16[384,640]{1,0:T(8,128)(2,1)S(1)}, u32[]{:S(2)}, u32[]{:S(2)}) %collective-permute-start) | collective-permute-done | bytes 491552 | tf_op jit(solution)/shard_map/ppermute | solution.py:1082
  23.6 0.8 copy-done.3
  24.4 79.5 %forward.1 = (bf16[320,960]{1,0:T(8,128)(2,1)}, bf16[15,320,128]{2,1,0:T(8,128)(2,1)}, bf16[4,320,640]{2,1,0:T(8,128)(2,1)}, f32[5,1,960]{2,1,0:T(1,128)}, bf16[...) custom-call(bf16[320,960]{1,0:T(8,128)(2,1)} %bitcast.49, ...), custom_call_target="tpu_custom_call" | custom-call | flops 97749999616 | bytes 1048576 | tf_op jit(solution)/shard_map/forward/pallas_call | solution.py:375
  104.0 38.0 %ffn_second.1 = (bf16[320,960]{1,0:T(8,128)(2,1)}, f32[320,960]{1,0:T(8,128)}, f32[8,960]{1,0:T(8,128)}, bf16[3,4,2,120,640]{4,3,2,1,0:T(8,128)(2,1)}) custom-call(bf16[320,960]{1,0:T(8,128)(2,1)} %bitcast.48, bf16[320,960]{1,0:T(8,128)(2,1)} %get-tuple-element.48.refs_1_, f32[320,960]{1,0:T(8,128)} %get-tuple-element.49.refs_2_, ...), custom_call_target="tpu_custom_call" | custom-call | flops 34500001792 | bytes 1048576 | tf_op jit(solution)/shard_map/ffn_second/pallas_call | solution.py:612
  142.0 33.4 %attn_backward.1 = (f32[320,960]{1,0:T(8,128)}, f32[8,960]{1,0:T(8,128)}, bf16[8,128,960]{2,1,0:T(8,128)(2,1)}, bf16[8,128,960]{2,1,0:T(8,128)(2,1)}, bf16[8,128,640]{2,1,0:T(8,128)(2,1)}) custom-call(f32[8,960]{1,0:T(8,128)} %get-tuple-element.53.gain_ref, f32[8,960]{1,0:T(8,128)} %select_maximum_fusion.gains_ref.refs_3_.refs_2_, s32[8,960]{1,0:T(8,128)} %pad.9.place_ref, ...), custom_call_target="tpu_custom_call" | custom-call | flops 46000001024 | bytes 1048576 | tf_op jit(solution)/shard_map/attn_backward/pallas_call | solution.py:1038
  175.3 45.2 %ffn_first_backward.1 = (f32[320,960]{1,0:T(8,128)}, f32[8,960]{1,0:T(8,128)}, bf16[3,4,2,120,640]{4,3,2,1,0:T(8,128)(2,1)}, bf16[4,120,640]{2,1,0:T(8,128)(2,1)}) custom-call(f32[320,960]{1,0:T(8,128)} %get-tuple-element.61.refs_0_, f32[320,960]{1,0:T(8,128)} %get-tuple-element.62.refs_1_, f32[8,960]{1,0:T(8,128)} %select_maximum_fusion.gains_ref.refs_3_.refs_2_, ...), custom_call_target="tpu_custom_call" | custom-call | flops 34500001792 | bytes 1048576 | tf_op jit(solution)/shard_map/ffn_first_backward/pallas_call | solution.py:612
  220.6 77.8 %attn_backward_last.1 = (f32[320,960]{1,0:T(8,128)}, f32[8,960]{1,0:T(8,128)}, f32[3,120,640]{2,1,0:T(8,128)}, f32[128,960]{1,0:T(8,128)}, f32[128,960]{1,0:T(8,128)}, /*index=5*/f32[128,640]{1,0:T(8,128)}) custom-call(f32[8,960]{1,0:T(8,128)} %get-tuple-element.67.gain_ref, f32[8,960]{1,0:T(8,128)} %select_maximum_fusion.gains_ref.refs_3_.refs_2_, ...), custom_call_target="tpu_custom_call" | custom-call | flops 109250002944 | bytes 1048576 | tf_op jit(solution)/shard_map/attn_backward_last/pallas_call | solution.py:1038
  298.4 0.8 constant_dynamic-slice_fusion
  299.3 0.5 slice_bitcast_fusion.3
  299.8 1.0 slice.32
  301.0 0.7 fusion.5
  301.8 0.8 slice.31
  302.6 0.8 slice.35
  303.4 0.9 slice_bitcast_fusion
  304.4 0.8 copy.28
  305.2 1.1 copy.29
  (35 shorter events, 0.7 us)
Async XLA Ops:
  7.2 5.2 %copy-start.6 = (s32[1,320]{1,0:T(1,128)S(1)}, s32[1,320]{1,0:T(1,128)}, u32[]{:S(2)}) copy-start(s32[1,320]{1,0:T(1,128)} %param.14) | copy-start | bytes 3844
  7.2 6.9 %copy-start.7 = (f32[960]{0:T(1024)S(1)}, f32[960]{0:T(1024)}, u32[]{:S(2)}) copy-start(f32[960]{0:T(1024)} %param.20) | copy-start | bytes 11524
  7.2 6.9 %copy-start.8 = (f32[960]{0:T(1024)S(1)}, f32[960]{0:T(1024)}, u32[]{:S(2)}) copy-start(f32[960]{0:T(1024)} %param.15) | copy-start | bytes 11524
  7.2 96.8 %all-gather.3.cloned.1.call-start = ((), (), s32[]{:S(2)}) async-start(), calls=%async_computation | async-start | bytes 4423680 | tf_op jit(solution)/shard_map/all_gather | solution.py:1092
  9.4 14.2 %collective-permute-start = (bf16[384,640]{1,0:T(8,128)(2,1)S(1)}, bf16[384,640]{1,0:T(8,128)(2,1)S(1)}, u32[]{:S(2)}, u32[]{:S(2)}) collective-permute-start(bf16[384,640]{1,0:T(8,128)(2,1)S(1)} %pad_maximum_fusion.1), channel_id=1, source_target_pairs={{0,16},{8,24},{16,0},{24,8},{1,17},{9,25},{17,1},{25,9},{2,18},{10... | collective-permute-start | bytes 1474568 | tf_op jit(solution)/shard_map/ppermute | solution.py:1082
  23.6 0.8 copy-start.3
  298.4 3.3 %copy-start.5 = (f32[128,960]{1,0:T(8,128)S(1)}, f32[128,960]{1,0:T(8,128)}, u32[]{:S(2)}) copy-start(f32[128,960]{1,0:T(8,128)} %get-tuple-element.81) | copy-start | bytes 1474564
  299.8 2.8 copy-start.4
  301.0 2.4 copy-start.1
  302.6 1.8 copy-start.2
  303.4 1.8 copy-start
Sparse Core Ops, SparseCore 0:
  24.5 71.5 all-gather.2

commit v4 on v3

--- a/solution.py
+++ b/solution.py
@@ -924,12 +924,14 @@
         early.finish()
         return
 
-    partners = [mate, x_mate, y_mate, near_z, far_z]
-    gain_hop = lambda n: hop(gain_out, gain_recv.at[n], partners[n])
-
-    def gain_add(n, copy):
-        copy.wait()
-        gain_out[...] += gain_recv[n]
+    stages = [((0, mate), (1, x_mate), (2, cross)), ((3, y_mate),), ((4, near_z),), ((5, far_z),)]
+    gain_hop = lambda n: [hop(gain_out, gain_recv.at[slot], target) for slot, target in stages[n]]
+
+    def gain_add(n, copies):
+        for copy in copies:
+            copy.wait()
+        for slot, _ in stages[n]:
+            gain_out[...] += gain_recv[slot]
 
     gain_copy = gain_hop(0)
     f_finish(2)
@@ -950,11 +952,9 @@
     kv_z = z_start(2, kv_y)
     q_z = z_next(1, q_z)
     gain_add(3, gain_copy)
-    gain_copy = gain_hop(4)
     f_finish(1)
     kv_z = z_next(2, kv_z)
     q_s = share_start(1, q_z)
-    gain_add(4, gain_copy)
     kv_s = share_start(2, kv_z)
     share_finish(0, o_s)
     share_finish(1, q_s)
@@ -1003,7 +1003,7 @@
         args = args + tuple(final)
         specs = specs + [ANYWHERE] * 5
         shapes = shapes + (((3, share, hidden), FULL),) + tuple(((4 * ROWS_PAD, c), FULL) for c in sizes)
-        hops = 3 + 2 + 6 + 5 + 3 * (2 + 1 + 1 + 2 + 3)
+        hops = 3 + 2 + 6 + 6 + 3 * (2 + 1 + 1 + 2 + 3)
         scratch += [pltpu.SemaphoreType.DMA((hops,))] * 2
         out_specs = out_specs + (ANYWHERE,) * 4
         scratch += [pltpu.VMEM(*s) for s in part_shapes]
@@ -1014,7 +1014,7 @@
             pltpu.VMEM((3, 2, share, hidden), LOW),
             pltpu.VMEM((3, share, hidden), LOW),
             pltpu.VMEM((3, share, hidden), LOW),
-            pltpu.VMEM((5, 8, width), FULL),
+            pltpu.VMEM((6, 8, width), FULL),
         ]
         scratch += [pltpu.VMEM(*s) for s in part_shapes]
         scratch += [pltpu.VMEM(*s) for s in shapes[2:]]

time: 318 us -> 326 us (1.025)
  Pallas kernels: 274 us -> 283 us
    pallas_call x2, Pallas kernels: 111 us -> 120 us  [attn_backward(): pl.pallas_call(functools.partial(attn_backward_kernel, last), out_shape=t...]
where the time goes in v4:
time: 326 us; the launch traced here: 322 us
  Pallas kernels  283 us (87%)
  between operations  14.7 us (5%)
  local copies, waits for them, and re-layouts  11.6 us (4%)
  waiting for transfers between devices  7.69 us (2%)
    pallas_call x2, Pallas kernels, attn_backward(): pl.pallas_call(functools.partial(attn_backward_kernel, last), out_shape=t...  120 us
    pallas_call x2, Pallas kernels, ffn_all(): pl.pallas_call(functools.partial(ffn_all_call, len(stills), second, reduc...  83.2 us
    pallas_call x1, Pallas kernels, forward(): pl.pallas_call(forward_kernel, out_shape=tuple((jax.ShapeDtypeStruct(*s)...  79.5 us
    ppermute x1, waiting for transfers between devices, over_x(): return lax.ppermute(value, 'seq', [(s, (s + 2) % 4) for s in range(4)])  7.66 us
  transfers between devices with their start and end apart: 2, of which 1 were waited for; matrix products, arithmetic and copies ran while one was open for 1% of the time, Pallas kernels for 25%

profile of v4, /device:TPU:0, one launch (start us, length us, event | category | flops | bytes accessed | tf_op | source)
XLA Modules:
  0.0 322.3 jit_solution(17992301332529959071)
XLA Ops:
  7.3 1.0 dynamic-slice_bitcast_fusion
  8.2 1.1 constant_dynamic-slice_fusion.1
  9.4 3.0 collective-permute-start
  12.7 0.6 multiply_cosine_fusion
  13.5 0.6 pad.9.place_ref
  14.1 0.6 select_maximum_fusion.gains_ref.refs_3_.refs_2_
  14.8 0.3 maximum_bitcast_fusion
  15.1 0.9 pad_maximum_fusion.trig_hbm
  16.0 7.7 %collective-permute-done = bf16[384,640]{1,0:T(8,128)(2,1)S(1)} collective-permute-done((bf16[384,640]{1,0:T(8,128)(2,1)S(1)}, bf16[384,640]{1,0:T(8,128)(2,1)S(1)}, u32[]{:S(2)}, u32[]{:S(2)}) %collective-permute-start) | collective-permute-done | bytes 491552 | tf_op jit(solution)/shard_map/ppermute | solution.py:1082
  23.6 0.8 copy-done.3
  24.4 79.5 %forward.1 = (bf16[320,960]{1,0:T(8,128)(2,1)}, bf16[15,320,128]{2,1,0:T(8,128)(2,1)}, bf16[4,320,640]{2,1,0:T(8,128)(2,1)}, f32[5,1,960]{2,1,0:T(1,128)}, bf16[...) custom-call(bf16[320,960]{1,0:T(8,128)(2,1)} %bitcast.49, ...), custom_call_target="tpu_custom_call" | custom-call | flops 97749999616 | bytes 1048576 | tf_op jit(solution)/shard_map/forward/pallas_call | solution.py:375
  104.0 38.0 %ffn_second.1 = (bf16[320,960]{1,0:T(8,128)(2,1)}, f32[320,960]{1,0:T(8,128)}, f32[8,960]{1,0:T(8,128)}, bf16[3,4,2,120,640]{4,3,2,1,0:T(8,128)(2,1)}) custom-call(bf16[320,960]{1,0:T(8,128)(2,1)} %bitcast.48, bf16[320,960]{1,0:T(8,128)(2,1)} %get-tuple-element.48.refs_1_, f32[320,960]{1,0:T(8,128)} %get-tuple-element.49.refs_2_, ...), custom_call_target="tpu_custom_call" | custom-call | flops 34500001792 | bytes 1048576 | tf_op jit(solution)/shard_map/ffn_second/pallas_call | solution.py:612
  142.0 33.4 %attn_backward.1 = (f32[320,960]{1,0:T(8,128)}, f32[8,960]{1,0:T(8,128)}, bf16[8,128,960]{2,1,0:T(8,128)(2,1)}, bf16[8,128,960]{2,1,0:T(8,128)(2,1)}, bf16[8,128,640]{2,1,0:T(8,128)(2,1)}) custom-call(f32[8,960]{1,0:T(8,128)} %get-tuple-element.53.gain_ref, f32[8,960]{1,0:T(8,128)} %select_maximum_fusion.gains_ref.refs_3_.refs_2_, s32[8,960]{1,0:T(8,128)} %pad.9.place_ref, ...), custom_call_target="tpu_custom_call" | custom-call | flops 46000001024 | bytes 1048576 | tf_op jit(solution)/shard_map/attn_backward/pallas_call | solution.py:1038
  175.3 45.2 %ffn_first_backward.1 = (f32[320,960]{1,0:T(8,128)}, f32[8,960]{1,0:T(8,128)}, bf16[3,4,2,120,640]{4,3,2,1,0:T(8,128)(2,1)}, bf16[4,120,640]{2,1,0:T(8,128)(2,1)}) custom-call(f32[320,960]{1,0:T(8,128)} %get-tuple-element.61.refs_0_, f32[320,960]{1,0:T(8,128)} %get-tuple-element.62.refs_1_, f32[8,960]{1,0:T(8,128)} %select_maximum_fusion.gains_ref.refs_3_.refs_2_, ...), custom_call_target="tpu_custom_call" | custom-call | flops 34500001792 | bytes 1048576 | tf_op jit(solution)/shard_map/ffn_first_backward/pallas_call | solution.py:612
  220.6 86.5 %attn_backward_last.1 = (f32[320,960]{1,0:T(8,128)}, f32[8,960]{1,0:T(8,128)}, f32[3,120,640]{2,1,0:T(8,128)}, f32[128,960]{1,0:T(8,128)}, f32[128,960]{1,0:T(8,128)}, /*index=5*/f32[128,640]{1,0:T(8,128)}) custom-call(f32[8,960]{1,0:T(8,128)} %get-tuple-element.67.gain_ref, f32[8,960]{1,0:T(8,128)} %select_maximum_fusion.gains_ref.refs_3_.refs_2_, ...), custom_call_target="tpu_custom_call" | custom-call | flops 109250002944 | bytes 1048576 | tf_op jit(solution)/shard_map/attn_backward_last/pallas_call | solution.py:1038
  307.1 0.8 constant_dynamic-slice_fusion
  308.0 0.5 slice_bitcast_fusion.3
  308.5 1.0 slice.32
  309.7 0.7 fusion.5
  310.5 0.8 slice.31
  311.3 0.8 slice.35
  312.1 0.9 slice_bitcast_fusion
  313.1 0.8 copy.28
  313.9 1.1 copy.29
  (35 shorter events, 0.7 us)
Async XLA Ops:
  7.2 5.2 %copy-start.6 = (s32[1,320]{1,0:T(1,128)S(1)}, s32[1,320]{1,0:T(1,128)}, u32[]{:S(2)}) copy-start(s32[1,320]{1,0:T(1,128)} %param.14) | copy-start | bytes 3844
  7.2 6.9 %copy-start.7 = (f32[960]{0:T(1024)S(1)}, f32[960]{0:T(1024)}, u32[]{:S(2)}) copy-start(f32[960]{0:T(1024)} %param.20) | copy-start | bytes 11524
  7.2 6.9 %copy-start.8 = (f32[960]{0:T(1024)S(1)}, f32[960]{0:T(1024)}, u32[]{:S(2)}) copy-start(f32[960]{0:T(1024)} %param.15) | copy-start | bytes 11524
  7.2 96.8 %all-gather.3.cloned.1.call-start = ((), (), s32[]{:S(2)}) async-start(), calls=%async_computation | async-start | bytes 4423680 | tf_op jit(solution)/shard_map/all_gather | solution.py:1092
  9.4 14.2 %collective-permute-start = (bf16[384,640]{1,0:T(8,128)(2,1)S(1)}, bf16[384,640]{1,0:T(8,128)(2,1)S(1)}, u32[]{:S(2)}, u32[]{:S(2)}) collective-permute-start(bf16[384,640]{1,0:T(8,128)(2,1)S(1)} %pad_maximum_fusion.1), channel_id=1, source_target_pairs={{0,16},{8,24},{16,0},{24,8},{1,17},{9,25},{17,1},{25,9},{2,18},{10... | collective-permute-start | bytes 1474568 | tf_op jit(solution)/shard_map/ppermute | solution.py:1082
  23.6 0.8 copy-start.3
  307.1 3.3 %copy-start.5 = (f32[128,960]{1,0:T(8,128)S(1)}, f32[128,960]{1,0:T(8,128)}, u32[]{:S(2)}) copy-start(f32[128,960]{1,0:T(8,128)} %get-tuple-element.81) | copy-start | bytes 1474564
  308.5 2.8 copy-start.4
  309.7 2.4 copy-start.1
  311.3 1.8 copy-start.2
  312.1 1.8 copy-start
Sparse Core Ops, SparseCore 0:
  24.5 71.5 all-gather.2
